TPU v7x, 512 devices: a whole 4x8x8 slice. The times are simulated.
512 devices in a mesh: blk: 32 (over x_hi, z, core), adp: 16 (over y, x_lo).
Axes of the slice: x: 4 (x_hi: 2, x_lo: 2; x = x_hi * 2 + x_lo), y: 8, z: 8, core: 2. Of those that a mesh axis runs over, the one named last changes fastest.
Arguments:
- stream: bfloat16 [16384, 1536], P(('blk', 'adp')), may hold values from -6 to 6
- prenorm_gain: float32 [1536], replicated, may hold values from 0.25 to 1.75
- gate_up_weight: bfloat16 [2, 4608, 1536], P(None, 'blk'), may hold values from -0.15625 to 0.15625
- down_weight: bfloat16 [4608, 1536], P('blk'), may hold values from -0.09375 to 0.09375
- adapter_gate_input: bfloat16 [64, 32, 1536], P('adp'), may hold values from -0.15625 to 0.15625
- adapter_gate_output: bfloat16 [64, 2, 16, 4608], P('adp', None, None, 'blk'), may hold values from -0.75 to 0.75
- adapter_down_input: bfloat16 [64, 4608, 16], P('adp', 'blk'), may hold values from -0.09375 to 0.09375
- adapter_down_output: bfloat16 [64, 16, 1536], P('adp'), may hold values from -0.75 to 0.75
- adapter_of_request: int32 [256], replicated, may hold values from 0 to 63, as said below
- request_of_slot: int32 [16384], P(('blk', 'adp')), may hold values from 0 to 255
Outputs:
- mixed: bfloat16 [16384, 1536], P(('blk', 'adp'))
Inputs may be any that keep to these rules, and one draw needn't show every extreme that they name: `adapter_of_request`: exactly 16 distinct adapter numbers occur.
All inputs are finite; a program needn't handle non-finite values.
Results may differ from a plain program's by a relative error of at most 0.014.
Values may be sent and summed in bfloat16 or wider, within the bound.
A program may use at most 64 MiB of HBM per device.

v0:
```python
import jax
import jax.numpy as jnp
from jax import lax
from jax.sharding import PartitionSpec as P

ACTIVE = 16


norm_eps = 1e-06


def normalize(rows, gain):
    value_rows = rows.astype(jnp.float32)
    scale = lax.rsqrt(jnp.mean(value_rows * value_rows, axis=-1, keepdims=True) + norm_eps)
    return (value_rows * scale * gain).astype(jnp.bfloat16)


def local(
    stream,
    prenorm_gain,
    gate_up_weight,
    down_weight,
    adapter_gate_input,
    adapter_gate_output,
    adapter_down_input,
    adapter_down_output,
    adapter_of_request,
    request_of_slot,
):
    width = stream.shape[1]
    tok_rows = stream.shape[0]
    hidden_dev = down_weight.shape[0]
    rank_columns = adapter_down_output.shape[1]
    holders = lax.axis_size("adp")
    kept_rows = adapter_gate_input.shape[0]
    catalog = jnp.arange(kept_rows * holders, dtype=jnp.int32)
    used = jnp.any(adapter_of_request[:, None] == catalog[None, :], axis=0)
    order = jnp.cumsum(used.astype(jnp.int32)) - 1
    active_pos = jnp.arange(ACTIVE, dtype=jnp.int32)
    picked = used[None, :] & (order[None, :] == active_pos[:, None])
    active = jnp.sum(jnp.where(picked, catalog[None, :], 0), axis=1)
    every = (
        lax.all_gather(adapter_gate_input, "adp", axis=0, tiled=True),
        lax.all_gather(adapter_gate_output, "adp", axis=0, tiled=True),
        lax.all_gather(adapter_down_input, "adp", axis=0, tiled=True),
        lax.all_gather(adapter_down_output, "adp", axis=0, tiled=True),
    )
    input_factor = jnp.take(every[0], active, axis=0)
    output_factor = jnp.take(every[1], active, axis=0)
    down_input_factor = jnp.take(every[2], active, axis=0)
    down_output_factor = jnp.take(every[3], active, axis=0)
    table = jnp.arange(adapter_of_request.shape[0], dtype=jnp.int32)
    own_adapter = jnp.sum(
        jnp.where(request_of_slot[:, None] == table[None, :], adapter_of_request[None, :], 0),
        axis=1,
    )
    own_match = own_adapter[:, None] == active[None, :]
    own_slot = jnp.sum(jnp.where(own_match, active_pos[None, :], 0), axis=1)
    normed = normalize(stream, prenorm_gain)
    projected = jnp.einsum("td,ard->tar", normed, input_factor, preferred_element_type=jnp.float32)
    lowrank_input = jnp.sum(projected * own_match[:, :, None].astype(jnp.float32), axis=1).astype(
        jnp.bfloat16
    )
    all_rows, all_low, all_slot = (
        lax.all_gather(normed, "blk", axis=0, tiled=True),
        lax.all_gather(lowrank_input, "blk", axis=0, tiled=True),
        lax.all_gather(own_slot.astype(jnp.bfloat16), "blk", axis=0, tiled=True),
    )
    group_match = (
        all_slot.astype(jnp.float32)[:, None] == active_pos.astype(jnp.float32)[None, :]
    ).astype(jnp.bfloat16)
    base_output = lax.dot_general(
        all_rows,
        gate_up_weight.reshape(2 * hidden_dev, width),
        (((1,), (1,)), ((), ())),
        preferred_element_type=jnp.float32,
    )
    base_output = base_output.reshape(-1, 2, hidden_dev)
    spread_rows = (all_low[:, None, :] * group_match[:, :, None]).reshape(
        -1, ACTIVE, 2, rank_columns
    )
    adapter_delta = jnp.einsum(
        "kbpz,bpze->kpe", spread_rows, output_factor, preferred_element_type=jnp.float32
    )
    prenorm_input = base_output + adapter_delta
    hidden = (jax.nn.gelu(prenorm_input[:, 0], approximate=True) * prenorm_input[:, 1]).astype(
        jnp.bfloat16
    )
    down_total = lax.psum_scatter(
        jnp.dot(hidden, down_weight, preferred_element_type=jnp.float32).astype(jnp.bfloat16),
        "blk",
        scatter_dimension=0,
        tiled=True,
    ).astype(jnp.float32)
    partial_value = jnp.einsum(
        "tf,afr->tar", hidden, down_input_factor, preferred_element_type=jnp.float32
    )
    low_part = jnp.sum(partial_value * group_match.astype(jnp.float32)[:, :, None], axis=1)
    lowrank_down = lax.psum_scatter(
        low_part.astype(jnp.bfloat16), "blk", scatter_dimension=0, tiled=True
    )
    own_spread = (lowrank_down[:, None, :] * own_match.astype(jnp.bfloat16)[:, :, None]).reshape(
        tok_rows, ACTIVE * rank_columns
    )
    adapter_output = jnp.dot(
        own_spread,
        down_output_factor.reshape(ACTIVE * rank_columns, width),
        preferred_element_type=jnp.float32,
    )
    return (stream.astype(jnp.float32) + down_total + adapter_output).astype(jnp.bfloat16)


def solution(mesh):
    in_specs = (
        P(("blk", "adp"), None),
        P(),
        P(None, "blk", None),
        P("blk", None),
        P("adp", None, None),
        P("adp", None, None, "blk"),
        P("adp", "blk", None),
        P("adp", None, None),
        P(),
        P(("blk", "adp")),
    )
    out_specs = P(("blk", "adp"), None)
    return jax.shard_map(local, mesh=mesh, in_specs=in_specs, out_specs=out_specs, check_vma=False)
```

profile of v0, /device:TPU:6, one launch (start us, length us, event | category | flops | bytes accessed | tf_op | source)
XLA Modules:
  0.0 632.8 jit_solution(11934340288619031208)
XLA Ops:
  6.5 0.7 all-gather.6.cloned.1.call-update
  7.3 0.0 all-gather.4.cloned.1.call-start
  7.3 1.0 fusion.34
  8.3 1.6 fusion.36
  10.0 0.0 all-gather.4.cloned.1.call-update
  10.0 0.0 all-gather.8.cloned.1.call-start
  10.0 0.7 all-gather.8.cloned.1.call-update
  10.7 0.0 reduce-scatter.7.cloned.1.call-start
  10.8 0.8 fusion.40
  11.6 0.1 copy.21
  11.7 0.1 reduce-window.8
  11.8 0.1 add_reduce_fusion
  11.9 0.1 select_reduce_fusion.1
  12.0 0.9 select_reduce_fusion
  12.9 0.1 fusion.43
  13.0 1.3 dynamic-slice
  14.9 0.2 dynamic-update-slice
  15.2 76.0 %all-reduce = bf16[1024]{0:T(1024)(128)(2,1)S(1)} all-reduce(bf16[1024]{0:T(1024)(128)(2,1)S(1)} %dynamic-update-slice), channel_id=1, replica_groups=mesh['blk'=32,'adp'=16] {'blk'}, use_global_device_ids=true, to_apply=%add | all-reduce | flops 1024 | bytes 4096
  91.2 65.2 %all_gather.22 = bf16[64,2,16,144]{3,2,1,0:T(8,128)(2,1)S(1)} all-gather(bf16[4,2,16,144]{3,2,1,0:T(8,128)(2,1)} %param.15), channel_id=1, replica_groups=mesh['blk'=32,'adp'=16] {'adp'}, dimensions={0}, use_global_device_ids=true | all-gather | bytes 626688 | tf_op jit(solution)/shard_map/all_gather | solution.py:44
  156.4 1.3 gather_fusion
  157.7 41.0 %all_gather.26 = bf16[64,144,16]{1,2,0:T(8,128)(2,1)S(1)} all-gather(bf16[4,144,16]{1,2,0:T(8,128)(2,1)S(1)} %copy-done.5), channel_id=1, replica_groups=mesh['blk'=32,'adp'=16] {'adp'}, dimensions={0}, use_global_device_ids=true | all-gather | bytes 313344 | tf_op jit(solution)/shard_map/all_gather | solution.py:45
  198.6 0.6 gather_fusion.2
  199.2 0.1 compare_convert_fusion.1
  199.3 0.1 fusion.45
  199.4 0.1 broadcast_select_fusion
  199.5 0.0 copy-start.3
  199.5 0.0 all-gather.6.cloned.1.call-done
  199.5 3.5 gather_fusion.1
  203.0 1.4 fusion.13
  204.4 38.9 %all_gather.24 = bf16[1024,32]{1,0:T(8,128)(2,1)S(1)} all-gather(bf16[32,32]{1,0:T(8,128)(2,1)S(1)} %fusion.13), channel_id=1, replica_groups=mesh['blk'=32,'adp'=16] {'blk'}, dimensions={0}, use_global_device_ids=true | all-gather | bytes 67584 | tf_op jit(solution)/shard_map/all_gather | solution.py:66
  243.3 0.1 copy.22
  243.4 0.4 convolution_bitcast_fusion.1
  243.9 38.0 %all-gather.4.cloned.1.call-done = bf16[1024,1536]{1,0:T(8,128)(2,1)} async-done(((bf16[32,1536]{1,0:T(8,128)(2,1)}), bf16[1024,1536]{1,0:T(8,128)(2,1)}) %all-gather.4.cloned.1.call-update) | async-done | bytes 3145744 | tf_op jit(solution)/shard_map/all_gather | solution.py:65
  281.8 3.0 fusion.7
  284.9 0.2 fusion.28
  285.1 0.3 fusion.50
  285.4 0.1 multiply_reduce_fusion
  285.5 0.9 copy.23
  286.3 0.0 reduce-scatter.7.cloned.1.call-update
  286.4 0.0 reduce-scatter.5.cloned.1.call-start
  286.4 2.7 convolution_convert_fusion
  289.1 0.0 reduce-scatter.5.cloned.1.call-update
  289.2 75.4 %all-gather.8.cloned.1.call-done = bf16[64,16,1536]{2,1,0:T(8,128)(2,1)} async-done(((bf16[4,16,1536]{2,1,0:T(8,128)(2,1)}), bf16[64,16,1536]{2,1,0:T(8,128)(2,1)}) %all-gather.8.cloned.1.call-update) | async-done | bytes 3145744 | tf_op jit(solution)/shard_map/all_gather | solution.py:46
  364.6 2.5 gather_fusion.3
  367.1 122.9 %reduce-scatter.7.cloned.1.call-done = bf16[32,16]{1,0:T(8,128)(2,1)} async-done(((bf16[1024,16]{1,0:T(8,128)(2,1)}), bf16[32,16]{1,0:T(8,128)(2,1)}) %reduce-scatter.7.cloned.1.call-update) | async-done | bytes 1040
  489.9 0.8 copy.24
  490.7 133.7 %reduce-scatter.5.cloned.1.call-done = bf16[32,1536]{1,0:T(8,128)(2,1)} async-done(((bf16[1024,1536]{1,0:T(8,128)(2,1)}), bf16[32,1536]{1,0:T(8,128)(2,1)}) %reduce-scatter.5.cloned.1.call-update) | async-done | bytes 98320 | tf_op jit(solution)/shard_map/reduce_scatter | solution.py:89
  624.4 1.9 fusion.3
  (21 shorter events, 0.1 us)
Async XLA Ops:
  6.5 275.3 %copy-start = (bf16[2,144,1536]{2,1,0:T(8,128)(2,1)S(1)}, bf16[2,144,1536]{2,1,0:T(8,128)(2,1)}, u32[]{:S(2)}) copy-start(bf16[2,144,1536]{2,1,0:T(8,128)(2,1)} %param.12) | copy-start | bytes 2654212
  6.5 151.1 %copy-start.5 = (bf16[4,144,16]{1,2,0:T(8,128)(2,1)S(1)}, bf16[4,144,16]{1,2,0:T(8,128)(2,1)}, u32[]{:S(2)}) copy-start(bf16[4,144,16]{1,2,0:T(8,128)(2,1)} %param.16) | copy-start | bytes 55300
  6.5 192.9 %all-gather.6.cloned.1.call-start = ((), (), s32[]{:S(2)}) async-start(), calls=%async_computation.3 | async-start | bytes 6684672 | tf_op jit(solution)/shard_map/all_gather | solution.py:43
  7.3 274.6 %all-gather.4.cloned.1.call-start = ((), (), s32[]{:S(2)}) async-start(), calls=%async_computation.2 | async-start | bytes 3244032 | tf_op jit(solution)/shard_map/all_gather | solution.py:65
  10.0 354.6 %all-gather.8.cloned.1.call-start = ((), (), s32[]{:S(2)}) async-start(), calls=%async_computation.5 | async-start | bytes 3342336 | tf_op jit(solution)/shard_map/all_gather | solution.py:46
  10.7 479.2 %reduce-scatter.7.cloned.1.call-start = ((), (), s32[]{:S(2)}) async-start(), calls=%async_computation.6 | async-start | bytes 270336
  199.5 3.5 copy-start.3
  203.0 40.4 %copy-start.4 = (bf16[16,2,16,144]{3,2,1,0:T(8,128)(2,1)S(1)}, bf16[16,2,16,144]{3,2,1,0:T(8,128)(2,1)}, u32[]{:S(2)}) copy-start(bf16[16,2,16,144]{3,2,1,0:T(8,128)(2,1)} %gather_fusion) | copy-start | bytes 442372
  285.1 1.4 copy-start.1
  286.4 338.0 %reduce-scatter.5.cloned.1.call-start = ((), (), s32[]{:S(2)}) async-start(), calls=%async_computation.4 | async-start | bytes 3244032 | tf_op jit(solution)/shard_map/reduce_scatter | solution.py:89
  289.2 335.3 %copy-start.2 = (bf16[32,1536]{1,0:T(8,128)(2,1)S(1)}, bf16[32,1536]{1,0:T(8,128)(2,1)}, u32[]{:S(2)}) copy-start(bf16[32,1536]{1,0:T(8,128)(2,1)} %param.10) | copy-start | bytes 294916
Sparse Core Ops, SparseCore 0:
  9.4 176.4 all-gather.5
  189.2 92.5 all-gather.3
  283.9 80.5 all-gather.7
  369.0 120.8 reduce-scatter.6
  494.5 129.8 reduce-scatter.4
where the time goes:
time: 634 us; the launch traced here: 633 us
  waiting for transfers between devices  371 us (59%)
  blocking collectives  221 us (35%)
  between operations  14 us (2%)
  local copies, waits for them, and re-layouts  11.2 us (2%)
  matrix products  9.7 us (2%)
    reduce_scatter x1, waiting for transfers between devices, local(): lax.psum_scatter(jnp.dot(hidden, down_weight, preferred_element_type=jnp....  134 us
    unnamed x6, waiting for transfers between devices  124 us
    unnamed x1, blocking collectives  76 us
    all_gather x1, waiting for transfers between devices, local(): lax.all_gather(adapter_down_output, 'adp', axis=0, tiled=True)  75.4 us
    all_gather x1, blocking collectives, local(): lax.all_gather(adapter_gate_output, 'adp', axis=0, tiled=True)  65.2 us
    all_gather x1, blocking collectives, local(): lax.all_gather(adapter_down_input, 'adp', axis=0, tiled=True)  41 us
    all_gather x1, blocking collectives, local(): lax.all_gather(lowrank_input, 'blk', axis=0, tiled=True)  38.9 us
    all_gather x1, waiting for transfers between devices, local(): lax.all_gather(normed, 'blk', axis=0, tiled=True)  38 us
  transfers between devices with their start and end apart: 5, of which 4 were waited for; matrix products, arithmetic and copies ran while one was open for 4% of the time, Pallas kernels for 0%

commit v1 on v0

--- a/solution.py
+++ b/solution.py
@@ -57,57 +57,54 @@
     own_match = own_adapter[:, None] == active[None, :]
     own_slot = jnp.sum(jnp.where(own_match, active_pos[None, :], 0), axis=1)
     normed = normalize(stream, prenorm_gain)
-    projected = jnp.einsum("td,ard->tar", normed, input_factor, preferred_element_type=jnp.float32)
-    lowrank_input = jnp.sum(projected * own_match[:, :, None].astype(jnp.float32), axis=1).astype(
-        jnp.bfloat16
+    packed = jnp.concatenate(
+        [normed, jnp.broadcast_to(own_slot.astype(jnp.bfloat16)[:, None], (tok_rows, 128))], axis=1
     )
-    all_rows, all_low, all_slot = (
-        lax.all_gather(normed, "blk", axis=0, tiled=True),
-        lax.all_gather(lowrank_input, "blk", axis=0, tiled=True),
-        lax.all_gather(own_slot.astype(jnp.bfloat16), "blk", axis=0, tiled=True),
+    gathered = lax.all_gather(packed, "blk", axis=0, tiled=True)
+    all_rows = gathered[:, :width]
+    group_match = gathered[:, width : width + 1].astype(jnp.float32) == active_pos.astype(
+        jnp.float32
     )
-    group_match = (
-        all_slot.astype(jnp.float32)[:, None] == active_pos.astype(jnp.float32)[None, :]
-    ).astype(jnp.bfloat16)
-    base_output = lax.dot_general(
-        all_rows,
-        gate_up_weight.reshape(2 * hidden_dev, width),
-        (((1,), (1,)), ((), ())),
+    match_ranks = jnp.repeat(group_match, rank_columns, axis=1)
+    cat_rows = ACTIVE * rank_columns
+
+    pre = []
+    for side in range(2):
+        rows_in = input_factor[:, side * rank_columns : (side + 1) * rank_columns]
+        low = lax.dot_general(
+            all_rows,
+            rows_in.reshape(cat_rows, width),
+            (((1,), (1,)), ((), ())),
+            preferred_element_type=jnp.float32,
+        )
+        low_spread = jnp.where(match_ranks, low, 0).astype(jnp.bfloat16)
+        base = lax.dot_general(
+            all_rows,
+            gate_up_weight[side],
+            (((1,), (1,)), ((), ())),
+            preferred_element_type=jnp.float32,
+        )
+        pre.append(
+            base
+            + jnp.dot(
+                low_spread,
+                output_factor[:, side].reshape(cat_rows, hidden_dev),
+                preferred_element_type=jnp.float32,
+            )
+        )
+    hidden = (jax.nn.gelu(pre[0], approximate=True) * pre[1]).astype(jnp.bfloat16)
+    down_in = down_input_factor.transpose(1, 0, 2).reshape(hidden_dev, cat_rows)
+    partial_value = jnp.dot(hidden, down_in, preferred_element_type=jnp.float32)
+    low_spread = jnp.where(match_ranks, partial_value, 0).astype(jnp.bfloat16)
+    part = jnp.dot(hidden, down_weight, preferred_element_type=jnp.float32) + jnp.dot(
+        low_spread,
+        down_output_factor.reshape(cat_rows, width),
         preferred_element_type=jnp.float32,
     )
-    base_output = base_output.reshape(-1, 2, hidden_dev)
-    spread_rows = (all_low[:, None, :] * group_match[:, :, None]).reshape(
-        -1, ACTIVE, 2, rank_columns
-    )
-    adapter_delta = jnp.einsum(
-        "kbpz,bpze->kpe", spread_rows, output_factor, preferred_element_type=jnp.float32
-    )
-    prenorm_input = base_output + adapter_delta
-    hidden = (jax.nn.gelu(prenorm_input[:, 0], approximate=True) * prenorm_input[:, 1]).astype(
-        jnp.bfloat16
-    )
-    down_total = lax.psum_scatter(
-        jnp.dot(hidden, down_weight, preferred_element_type=jnp.float32).astype(jnp.bfloat16),
-        "blk",
-        scatter_dimension=0,
-        tiled=True,
+    total = lax.psum_scatter(
+        part.astype(jnp.bfloat16), "blk", scatter_dimension=0, tiled=True
     ).astype(jnp.float32)
-    partial_value = jnp.einsum(
-        "tf,afr->tar", hidden, down_input_factor, preferred_element_type=jnp.float32
-    )
-    low_part = jnp.sum(partial_value * group_match.astype(jnp.float32)[:, :, None], axis=1)
-    lowrank_down = lax.psum_scatter(
-        low_part.astype(jnp.bfloat16), "blk", scatter_dimension=0, tiled=True
-    )
-    own_spread = (lowrank_down[:, None, :] * own_match.astype(jnp.bfloat16)[:, :, None]).reshape(
-        tok_rows, ACTIVE * rank_columns
-    )
-    adapter_output = jnp.dot(
-        own_spread,
-        down_output_factor.reshape(ACTIVE * rank_columns, width),
-        preferred_element_type=jnp.float32,
-    )
-    return (stream.astype(jnp.float32) + down_total + adapter_output).astype(jnp.bfloat16)
+    return (stream.astype(jnp.float32) + total).astype(jnp.bfloat16)
 
 
 def solution(mesh):

time: 634 us -> 530 us (0.84)
  blocking collectives: 221 us -> 107 us
  matrix products: 9.7 us -> 25.2 us
    all_gather x1, waiting for transfers between devices: 0.02 us -> 141 us  [local(): lax.all_gather(adapter_gate_input, 'adp', axis=0, tiled=True)]
    unnamed x6 -> x4, waiting for transfers between devices: 124 us -> 1.42 us
    unnamed x1 -> x0, blocking collectives: 76 us -> none
    all_gather x1, waiting for transfers between devices: 75.4 us -> 1.37 us  [local(): lax.all_gather(adapter_down_output, 'adp', axis=0, tiled=True)]
    all_gather x1, waiting for transfers between devices: 38 us -> 90.4 us  [local(): gathered = lax.all_gather(packed, 'blk', axis=0, tiled=True)]
    all_gather x1 -> x0, blocking collectives: 38.9 us -> none  [local(): lax.all_gather(lowrank_input, 'blk', axis=0, tiled=True)]
    dot_general x4 -> x5, matrix products: 6.71 us -> 19.7 us  [the longest x2 8.06 us: local(): jnp.dot(low_spread, output_factor[:, side].reshape(cat_rows, hidden_dev),...]
    all_gather x1, blocking collectives: 41 us -> 50.8 us  [local(): lax.all_gather(adapter_down_input, 'adp', axis=0, tiled=True)]
  transfers between devices with their start and end apart: 5 -> 4, of which waited for: 4 -> 4; matrix products, arithmetic and copies ran while one was open for 4% -> 2% of each run, Pallas kernels for 0% -> 0%
where the time goes in v1:
time: 530 us; the launch traced here: 528 us
  waiting for transfers between devices  367 us (69%)
  blocking collectives  107 us (20%)
  matrix products  25.2 us (5%)
  between operations  13.3 us (3%)
  other arithmetic  8.07 us (2%)
  local copies, waits for them, and re-layouts  7.92 us (1%)
    all_gather x1, waiting for transfers between devices, local(): lax.all_gather(adapter_gate_input, 'adp', axis=0, tiled=True)  141 us
    reduce_scatter x1, waiting for transfers between devices, local(): lax.psum_scatter(part.astype(jnp.bfloat16), 'blk', scatter_dimension=0, t...  133 us
    all_gather x1, waiting for transfers between devices, local(): gathered = lax.all_gather(packed, 'blk', axis=0, tiled=True)  90.4 us
    all_gather x1, blocking collectives, local(): lax.all_gather(adapter_gate_output, 'adp', axis=0, tiled=True)  55.9 us
    all_gather x1, blocking collectives, local(): lax.all_gather(adapter_down_input, 'adp', axis=0, tiled=True)  50.8 us
  transfers between devices with their start and end apart: 4, of which 4 were waited for; matrix products, arithmetic and copies ran while one was open for 2% of the time, Pallas kernels for 0%

profile of v1, /device:TPU:6, one launch (start us, length us, event | category | flops | bytes accessed | tf_op | source)
XLA Modules:
  0.0 528.5 jit_solution(233450659145894325)
XLA Ops:
  6.5 0.0 copy-start
  6.5 0.0 all-gather.8.cloned.1.call-start
  6.5 0.7 all-gather.8.cloned.1.call-update
  7.3 0.0 all-gather.4.cloned.1.call-start
  7.3 0.8 fusion.60
  8.1 0.1 copy.17
  8.2 0.1 reduce-window.8
  8.3 0.1 add_reduce_fusion
  8.4 0.1 select_reduce_fusion.2
  8.5 0.9 select_reduce_fusion
  9.4 0.1 select_reduce_fusion.1
  9.5 1.0 fusion.56
  10.5 1.0 fusion.58
  11.5 0.1 broadcast_in_dim.116
  11.6 0.7 pad_maximum_fusion
  12.3 0.0 all-gather.4.cloned.1.call-update
  12.3 0.0 all-gather.6.cloned.1.call-start
  12.3 0.7 all-gather.6.cloned.1.call-update
  13.0 0.0 reduce-scatter.2.cloned.1.call-start
  13.1 0.1 broadcast_in_dim.125
  13.2 0.1 broadcast_in_dim.126
  13.3 55.9 %all_gather.17 = bf16[64,2,16,144]{3,2,1,0:T(8,128)(2,1)S(1)} all-gather(bf16[4,2,16,144]{3,2,1,0:T(8,128)(2,1)} %param.15), channel_id=1, replica_groups=mesh['blk'=32,'adp'=16] {'adp'}, dimensions={0}, use_global_device_ids=true | all-gather | bytes 626688 | tf_op jit(solution)/shard_map/all_gather | solution.py:44
  69.2 0.6 gather_fusion.1
  69.8 50.8 %all_gather.18 = bf16[64,144,16]{1,2,0:T(8,128)(2,1)S(1)} all-gather(bf16[4,144,16]{1,2,0:T(8,128)(2,1)} %param.16), channel_id=1, replica_groups=mesh['blk'=32,'adp'=16] {'adp'}, dimensions={0}, use_global_device_ids=true | all-gather | bytes 313344 | tf_op jit(solution)/shard_map/all_gather | solution.py:45
  120.6 0.6 gather_fusion.2
  121.2 0.1 broadcast_select_fusion.2
  121.3 0.1 broadcast_select_fusion.1
  121.4 1.4 all-gather.8.cloned.1.call-done
  122.8 2.5 gather_fusion.3
  125.3 0.2 bitcast_select_fusion
  125.4 90.4 %all-gather.4.cloned.1.call-done = bf16[1024,1664]{1,0:T(8,128)(2,1)} async-done(((bf16[32,1664]{1,0:T(8,128)(2,1)}), bf16[1024,1664]{1,0:T(8,128)(2,1)}) %all-gather.4.cloned.1.call-update) | async-done | bytes 3407888 | tf_op jit(solution)/shard_map/all_gather | solution.py:63
  215.8 1.1 convert_reduce_fusion
  216.9 0.1 broadcast_compare_fusion
  217.0 0.1 broadcast_in_dim.117
  217.1 0.3 copy.18
  217.5 141.0 %all-gather.6.cloned.1.call-done = bf16[64,32,1536]{2,1,0:T(8,128)(2,1)} async-done(((bf16[4,32,1536]{2,1,0:T(8,128)(2,1)}), bf16[64,32,1536]{2,1,0:T(8,128)(2,1)}) %all-gather.6.cloned.1.call-update) | async-done | bytes 6291472 | tf_op jit(solution)/shard_map/all_gather | solution.py:43
  358.5 3.4 gather_fusion
  361.9 0.2 broadcast_select_fusion
  362.1 0.1 fusion.66
  362.2 4.0 fusion.34
  366.2 4.2 fusion.46
  370.4 4.1 fusion.31
  374.5 3.3 fusion.37
  377.8 4.1 fusion.36
  381.9 5.5 %add_convert_fusion = bf16[1024,1536]{1,0:T(8,128)(2,1)} fusion(f32[1024,1536]{1,0:T(8,128)} %fusion.36, bf16[1024,144]{0,1:T(8,128)(2,1)S(1)} %fusion.37, bf16[144,1536]{1,0:T(8,128)(2,1)S(1)} %copy-done), kind=kOutput, calls=%fused_computation.4 | convolution fusion | flops 456130560 | bytes 10174464 | tf_op jit(solution)/shard_map/dot_general | solution.py:99
  387.4 0.0 reduce-scatter.2.cloned.1.call-update
  387.5 132.9 %reduce-scatter.2.cloned.1.call-done = bf16[32,1536]{1,0:T(8,128)(2,1)} async-done(((bf16[1024,1536]{1,0:T(8,128)(2,1)}), bf16[32,1536]{1,0:T(8,128)(2,1)}) %reduce-scatter.2.cloned.1.call-update) | async-done | bytes 98320 | tf_op jit(solution)/shard_map/reduce_scatter | solution.py:104
  520.4 1.6 fusion.59
  (13 shorter events, 0.1 us)
Async XLA Ops:
  6.5 375.4 %copy-start = (bf16[144,1536]{1,0:T(8,128)(2,1)S(1)}, bf16[144,1536]{1,0:T(8,128)(2,1)}, u32[]{:S(2)}) copy-start(bf16[144,1536]{1,0:T(8,128)(2,1)} %param.13) | copy-start | bytes 1327108
  6.5 116.2 %all-gather.8.cloned.1.call-start = ((), (), s32[]{:S(2)}) async-start(), calls=%async_computation.3 | async-start | bytes 3342336 | tf_op jit(solution)/shard_map/all_gather | solution.py:46
  7.3 208.6 %all-gather.4.cloned.1.call-start = ((), (), s32[]{:S(2)}) async-start(), calls=%async_computation.1 | async-start | bytes 3514368 | tf_op jit(solution)/shard_map/all_gather | solution.py:63
  12.3 346.2 %all-gather.6.cloned.1.call-start = ((), (), s32[]{:S(2)}) async-start(), calls=%async_computation.2 | async-start | bytes 6684672 | tf_op jit(solution)/shard_map/all_gather | solution.py:43
  13.0 507.3 %reduce-scatter.2.cloned.1.call-start = ((), (), s32[]{:S(2)}) async-start(), calls=%async_computation.4 | async-start | bytes 3244032 | tf_op jit(solution)/shard_map/reduce_scatter | solution.py:104
  370.4 4.1 copy-start.2
  387.4 132.9 %copy-start.1 = (bf16[32,1536]{1,0:T(8,128)(2,1)S(1)}, bf16[32,1536]{1,0:T(8,128)(2,1)}, u32[]{:S(2)}) copy-start(bf16[32,1536]{1,0:T(8,128)(2,1)} %param.10) | copy-start | bytes 294916
Sparse Core Ops, SparseCore 0:
  9.4 113.2 all-gather.7
  126.1 89.6 all-gather.3
  217.9 140.4 all-gather.5
  387.6 132.7 reduce-scatter.1

commit v2 on v1

v2 whole, which is shorter than its diff:
```python
import jax
import jax.numpy as jnp
from jax import lax
from jax.experimental import pallas as pl
from jax.experimental.pallas import tpu as pltpu
from jax.sharding import PartitionSpec as P

ACTIVE = 16
RING = 8
FWD, BWD = 0, 1
OWN, OTHER = 0, 1

norm_eps = 1e-06


def normalize(rows, gain):
    value_rows = rows.astype(jnp.float32)
    scale = lax.rsqrt(jnp.mean(value_rows * value_rows, axis=-1, keepdims=True) + norm_eps)
    return (value_rows * scale * gain).astype(jnp.bfloat16)


def blk_index(x_hi, z, core):
    return x_hi * (2 * RING) + z * 2 + core


def greet(targets):
    barrier = pltpu.get_barrier_semaphore()
    for target in targets:
        pl.semaphore_signal(
            barrier, inc=1, device_id=target, device_id_type=pl.DeviceIdType.MESH
        )
    pl.semaphore_wait(barrier, len(targets))


def remote(src, dst, send_sem, recv_sem, target):
    return pltpu.make_async_remote_copy(
        src_ref=src,
        dst_ref=dst,
        send_sem=send_sem,
        recv_sem=recv_sem,
        device_id=target,
        device_id_type=pl.DeviceIdType.MESH,
    )


def adp_peers(holders):
    me = lax.axis_index("adp")
    return [{"adp": lax.rem(me + step, holders)} for step in range(1, holders)]


def adp_start(holders, own_ref, all_ref, send_sem, recv_sem):
    me = lax.axis_index("adp")
    copies = []
    for step, target in enumerate(adp_peers(holders)):
        copy = remote(own_ref, all_ref.at[me], send_sem.at[step], recv_sem.at[step], target)
        copy.start()
        copies.append(copy)
    return copies


def adp_finish(holders, copies, all_ref, recv_sem, send_sem):
    me = lax.axis_index("adp")
    for step, target in enumerate(adp_peers(holders)):
        source = lax.rem(me + holders - step - 1, holders)
        slab = all_ref.at[source]
        remote(slab, slab, send_sem.at[step], recv_sem.at[step], target).wait_recv()
    for copy in copies:
        copy.wait_send()


def adp_gather_kernel(holders, own_ref, all_ref, send_sem, recv_sem, local_sem):
    me = lax.axis_index("adp")
    greet(adp_peers(holders))
    copies = adp_start(holders, own_ref, all_ref, send_sem, recv_sem)
    keep = pltpu.make_async_copy(own_ref, all_ref.at[me], local_sem)
    keep.start()
    adp_finish(holders, copies, all_ref, recv_sem, send_sem)
    keep.wait()


def adp_gather(own, holders):
    def kernel(*refs):
        adp_gather_kernel(holders, *refs)

    return pl.pallas_call(
        kernel,
        out_shape=jax.ShapeDtypeStruct((holders,) + own.shape, own.dtype),
        in_specs=[pl.BlockSpec(memory_space=pltpu.VMEM)],
        out_specs=pl.BlockSpec(memory_space=pltpu.VMEM),
        scratch_shapes=[
            pltpu.SemaphoreType.DMA((holders - 1,)),
            pltpu.SemaphoreType.DMA((holders - 1,)),
            pltpu.SemaphoreType.DMA,
        ],
        compiler_params=pltpu.CompilerParams(collective_id=1, has_side_effects=True),
        name="adp_gather",
    )(own)


def reach(stream, way):
    return 4 if (stream == OWN) == (way == FWD) else 3


def rows_gather(own, factors, holders):
    blocks = 4 * RING

    def kernel(
        own_ref,
        factor_ref,
        all_ref,
        factor_all_ref,
        ring_send,
        ring_recv,
        across_send,
        across_recv,
        sib_send,
        sib_recv,
        adp_send,
        adp_recv,
        local_sem,
    ):
        me = lax.axis_index("blk")
        me_adp = lax.axis_index("adp")
        x_hi = me // (2 * RING)
        z = lax.rem(me // 2, RING)
        core = lax.rem(me, 2)
        sibling = {"blk": blk_index(x_hi, z, 1 - core)}
        across = {"blk": blk_index(1 - x_hi, z, core)}
        ahead = {
            FWD: {"blk": blk_index(x_hi, lax.rem(z + 1, RING), core)},
            BWD: {"blk": blk_index(x_hi, lax.rem(z + RING - 1, RING), core)},
        }
        greet([sibling, across, ahead[FWD], ahead[BWD]] + adp_peers(holders))
        sent = []

        def at(stream, way, far, owner_core):
            x_of = x_hi if stream == OWN else 1 - x_hi
            z_of = lax.rem(z + RING - far, RING) if way == FWD else lax.rem(z + far, RING)
            return blk_index(x_of, z_of, owner_core)

        def push(src, index, send_sem, recv_sem, target):
            copy = remote(src, all_ref.at[index], send_sem, recv_sem, target)
            copy.start()
            sent.append(copy)

        def to_ring(src, index, stream, way, far):
            push(
                src,
                index,
                ring_send.at[stream, way, far],
                ring_recv.at[stream, way, far],
                ahead[way],
            )

        def to_sibling(src, index, stream, way, far):
            push(
                src,
                index,
                sib_send.at[stream, way, far],
                sib_recv.at[stream, way, far],
                sibling,
            )

        push(own_ref, me, across_send, across_recv, across)
        to_ring(own_ref, me, OWN, FWD, 0)
        to_ring(own_ref, me, OWN, BWD, 0)
        to_sibling(own_ref, me, OWN, FWD, 0)
        adp_copies = adp_start(holders, factor_ref, factor_all_ref, adp_send, adp_recv)
        keep = pltpu.make_async_copy(own_ref, all_ref.at[me], local_sem.at[0])
        keep.start()
        keep_factor = pltpu.make_async_copy(factor_ref, factor_all_ref.at[me_adp], local_sem.at[1])
        keep_factor.start()

        other = at(OTHER, FWD, 0, core)
        slab = all_ref.at[other]
        remote(slab, slab, across_send, across_recv, across).wait_recv()
        to_ring(slab, other, OTHER, FWD, 0)
        to_ring(slab, other, OTHER, BWD, 0)
        to_sibling(slab, other, OTHER, FWD, 0)
        for far in range(1, 5):
            for stream in (OWN, OTHER):
                for way in (FWD, BWD):
                    last = reach(stream, way)
                    if far > last:
                        continue
                    index = at(stream, way, far, core)
                    slab = all_ref.at[index]
                    remote(
                        slab,
                        slab,
                        ring_send.at[stream, way, far - 1],
                        ring_recv.at[stream, way, far - 1],
                        ahead[way],
                    ).wait_recv()
                    if far < last:
                        to_ring(slab, index, stream, way, far)
                    to_sibling(slab, index, stream, way, far)
        for far in range(0, 5):
            for stream in (OWN, OTHER):
                for way in (FWD, BWD):
                    if far > reach(stream, way) or (far == 0 and way == BWD):
                        continue
                    slab = all_ref.at[at(stream, way, far, 1 - core)]
                    remote(
                        slab,
                        slab,
                        sib_send.at[stream, way, far],
                        sib_recv.at[stream, way, far],
                        sibling,
                    ).wait_recv()
        adp_finish(holders, adp_copies, factor_all_ref, adp_recv, adp_send)
        for copy in sent:
            copy.wait_send()
        keep.wait()
        keep_factor.wait()

    dma = pltpu.SemaphoreType.DMA
    return pl.pallas_call(
        kernel,
        out_shape=[
            jax.ShapeDtypeStruct((blocks,) + own.shape, own.dtype),
            jax.ShapeDtypeStruct((holders,) + factors.shape, factors.dtype),
        ],
        in_specs=[pl.BlockSpec(memory_space=pltpu.VMEM)] * 2,
        out_specs=[pl.BlockSpec(memory_space=pltpu.VMEM)] * 2,
        scratch_shapes=[
            dma((2, 2, 4)),
            dma((2, 2, 4)),
            dma,
            dma,
            dma((2, 2, 5)),
            dma((2, 2, 5)),
            dma((holders - 1,)),
            dma((holders - 1,)),
            dma((2,)),
        ],
        compiler_params=pltpu.CompilerParams(collective_id=2, has_side_effects=True),
        name="rows_gather",
    )(own, factors)


def sum_scatter(parts):
    rows, width = parts.shape[1:]

    def kernel(
        part_ref,
        out_ref,
        sib_ref,
        leave_ref,
        arrive_ref,
        cross_out_ref,
        cross_in_ref,
        ring_send,
        ring_recv,
        across_send,
        across_recv,
        sib_send,
        sib_recv,
    ):
        me = lax.axis_index("blk")
        x_hi = me // (2 * RING)
        z = lax.rem(me // 2, RING)
        core = lax.rem(me, 2)
        sibling = {"blk": blk_index(x_hi, z, 1 - core)}
        across = {"blk": blk_index(1 - x_hi, z, core)}
        ahead = {
            FWD: {"blk": blk_index(x_hi, lax.rem(z + 1, RING), core)},
            BWD: {"blk": blk_index(x_hi, lax.rem(z + RING - 1, RING), core)},
        }
        greet([sibling, across, ahead[FWD], ahead[BWD]])
        sent = []

        def at(stream, way, far, owner_core):
            x_of = x_hi if stream == OWN else 1 - x_hi
            z_of = lax.rem(z + far, RING) if way == FWD else lax.rem(z + RING - far, RING)
            return blk_index(x_of, z_of, owner_core)

        def push(copy):
            copy.start()
            sent.append(copy)

        order = []
        for far in range(4, -1, -1):
            for stream in (OTHER, OWN):
                for way in (FWD, BWD):
                    if far <= reach(stream, way) and not (far == 0 and way == BWD):
                        order.append((stream, way, far))

        def sib_copy(stream, way, far):
            return remote(
                part_ref.at[at(stream, way, far, 1 - core)],
                sib_ref.at[stream, way, far],
                sib_send.at[stream, way, far],
                sib_recv.at[stream, way, far],
                sibling,
            )

        for key in order:
            push(sib_copy(*key))

        def pair_sum(stream, way, far):
            sib_copy(stream, way, far).wait_recv()
            own = part_ref[at(stream, way, far, core)].astype(jnp.float32)
            return own + sib_ref[stream, way, far].astype(jnp.float32)

        def ring_copy(stream, way, far):
            return remote(
                leave_ref.at[stream, way, far - 1],
                arrive_ref.at[stream, way, far - 1],
                ring_send.at[stream, way, far - 1],
                ring_recv.at[stream, way, far - 1],
                ahead[way],
            )

        def arrived(stream, way, far):
            ring_copy(stream, way, far + 1).wait_recv()
            return arrive_ref[stream, way, far].astype(jnp.float32)

        totals = {}
        for key in order:
            stream, way, far = key
            total = pair_sum(*key)
            if far == 0:
                total = total + arrived(stream, FWD, 0) + arrived(stream, BWD, 0)
                if stream == OTHER:
                    cross_out_ref[...] = total.astype(cross_out_ref.dtype)
                    push(remote(cross_out_ref, cross_in_ref, across_send, across_recv, across))
                else:
                    totals[stream] = total
                continue
            if far < reach(stream, way):
                total = total + arrived(stream, way, far)
            leave_ref[stream, way, far - 1] = total.astype(leave_ref.dtype)
            push(ring_copy(stream, way, far))
        remote(cross_out_ref, cross_in_ref, across_send, across_recv, across).wait_recv()
        out_ref[...] = totals[OWN] + cross_in_ref[...].astype(jnp.float32)
        for copy in sent:
            copy.wait_send()

    dma = pltpu.SemaphoreType.DMA
    block = (rows, width)
    return pl.pallas_call(
        kernel,
        out_shape=jax.ShapeDtypeStruct(block, jnp.float32),
        in_specs=[pl.BlockSpec(memory_space=pltpu.VMEM)],
        out_specs=pl.BlockSpec(memory_space=pltpu.VMEM),
        scratch_shapes=[
            pltpu.VMEM((2, 2, 5) + block, parts.dtype),
            pltpu.VMEM((2, 2, 4) + block, parts.dtype),
            pltpu.VMEM((2, 2, 4) + block, parts.dtype),
            pltpu.VMEM(block, parts.dtype),
            pltpu.VMEM(block, parts.dtype),
            dma((2, 2, 4)),
            dma((2, 2, 4)),
            dma,
            dma,
            dma((2, 2, 5)),
            dma((2, 2, 5)),
        ],
        compiler_params=pltpu.CompilerParams(collective_id=3, has_side_effects=True),
        name="sum_scatter",
    )(parts)


def local(
    stream,
    prenorm_gain,
    gate_up_weight,
    down_weight,
    adapter_gate_input,
    adapter_gate_output,
    adapter_down_input,
    adapter_down_output,
    adapter_of_request,
    request_of_slot,
):
    width = stream.shape[1]
    tok_rows = stream.shape[0]
    hidden_dev = down_weight.shape[0]
    rank_columns = adapter_down_output.shape[1]
    holders = lax.axis_size("adp")
    kept_rows = adapter_gate_input.shape[0]
    catalog = jnp.arange(kept_rows * holders, dtype=jnp.int32)
    used = jnp.any(adapter_of_request[:, None] == catalog[None, :], axis=0)
    order = jnp.cumsum(used.astype(jnp.int32)) - 1
    active_pos = jnp.arange(ACTIVE, dtype=jnp.int32)
    picked = used[None, :] & (order[None, :] == active_pos[:, None])
    active = jnp.sum(jnp.where(picked, catalog[None, :], 0), axis=1)
    table = jnp.arange(adapter_of_request.shape[0], dtype=jnp.int32)
    own_adapter = jnp.sum(
        jnp.where(request_of_slot[:, None] == table[None, :], adapter_of_request[None, :], 0),
        axis=1,
    )
    own_match = own_adapter[:, None] == active[None, :]
    own_slot = jnp.sum(jnp.where(own_match, active_pos[None, :], 0), axis=1)
    normed = normalize(stream, prenorm_gain)
    place = lax.axis_index("blk")
    half = width // 2
    row_in = lax.dynamic_slice_in_dim(adapter_gate_input, place, 1, axis=1)[:, 0]
    row_out = lax.dynamic_slice(
        adapter_down_output, (0, place // 2, lax.rem(place, 2) * half), (kept_rows, 1, half)
    )[:, 0]
    catalog_rows = adp_gather(jnp.concatenate([row_in, row_out], axis=1), holders)
    choose = (active[:, None] == catalog[None, :]).astype(jnp.bfloat16)
    chosen = jnp.dot(
        choose, catalog_rows.reshape(-1, width + half), preferred_element_type=jnp.float32
    ).astype(jnp.bfloat16)
    tile_cols = half // 3
    packed = jnp.concatenate(
        [
            jnp.concatenate([normed, chosen[:, :width]], axis=0),
            jnp.concatenate(
                [chosen[:, width + k * tile_cols : width + (k + 1) * tile_cols] for k in range(3)],
                axis=0,
            ),
            jnp.concatenate(
                [
                    jnp.broadcast_to(own_slot.astype(jnp.bfloat16)[:, None], (tok_rows, 128)),
                    jnp.zeros((ACTIVE, 128), jnp.bfloat16),
                ],
                axis=0,
            ),
        ],
        axis=1,
    )
    own_factors = jnp.concatenate(
        [
            adapter_gate_output.reshape(kept_rows, 2 * rank_columns, hidden_dev),
            adapter_down_input.transpose(0, 2, 1),
        ],
        axis=1,
    )
    gathered, factors = rows_gather(packed, own_factors, holders)
    factors = jnp.take(
        factors.reshape(kept_rows * holders, 3 * rank_columns, hidden_dev), active, axis=0
    ).transpose(1, 0, 2)
    cat_rows = ACTIVE * rank_columns
    factors = factors.reshape(3, cat_rows, hidden_dev)
    all_rows = gathered[:, :tok_rows, :width].reshape(-1, width)
    rows_in = gathered[:, tok_rows:, :width].reshape(2, cat_rows, width)
    down_out = (
        gathered[:, :, width : width + tile_cols]
        .reshape(rank_columns, 2, 3, ACTIVE, tile_cols)
        .transpose(0, 3, 1, 2, 4)
        .reshape(cat_rows, width)
    )
    all_slot = gathered[:, :tok_rows, width + tile_cols].reshape(-1, 1).astype(jnp.int32)
    match = all_slot == (jnp.arange(cat_rows, dtype=jnp.int32) % ACTIVE)[None, :]
    contract_minor = (((1,), (1,)), ((), ()))
    pre = []
    for side in range(2):
        low = lax.dot_general(
            all_rows, rows_in[side], contract_minor, preferred_element_type=jnp.float32
        )
        base = lax.dot_general(
            all_rows, gate_up_weight[side], contract_minor, preferred_element_type=jnp.float32
        )
        low_spread = jnp.where(match, low, 0).astype(jnp.bfloat16)
        pre.append(base + jnp.dot(low_spread, factors[side], preferred_element_type=jnp.float32))
    hidden = (jax.nn.gelu(pre[0], approximate=True) * pre[1]).astype(jnp.bfloat16)
    low_part = lax.dot_general(
        hidden, factors[2], contract_minor, preferred_element_type=jnp.float32
    )
    low_spread = jnp.where(match, low_part, 0).astype(jnp.bfloat16)
    part = jnp.dot(hidden, down_weight, preferred_element_type=jnp.float32) + jnp.dot(
        low_spread, down_out, preferred_element_type=jnp.float32
    )
    total = sum_scatter(part.astype(jnp.bfloat16).reshape(-1, tok_rows, width))
    return (stream.astype(jnp.float32) + total).astype(jnp.bfloat16)


def solution(mesh):
    in_specs = (
        P(("blk", "adp"), None),
        P(),
        P(None, "blk", None),
        P("blk", None),
        P("adp", None, None),
        P("adp", None, None, "blk"),
        P("adp", "blk", None),
        P("adp", None, None),
        P(),
        P(("blk", "adp")),
    )
    out_specs = P(("blk", "adp"), None)
    return jax.shard_map(local, mesh=mesh, in_specs=in_specs, out_specs=out_specs, check_vma=False)
```

time: 530 us -> 151 us (0.28)
  the two profiles are of different devices: /device:TPU:6 before, /device:TPU:26 now
where the time goes in v2:
time: 151 us
  Pallas kernels  104 us (69%)
  matrix products  21.7 us (14%)
  local copies, waits for them, and re-layouts  14.7 us (10%)
  other arithmetic  10.3 us (7%)
    pallas_call x1, Pallas kernels, rows_gather(): pl.pallas_call(kernel, out_shape=[jax.ShapeDtypeStruct((blocks,) + own.sh...  57.2 us
    pallas_call x1, Pallas kernels, sum_scatter(): pl.pallas_call(kernel, out_shape=jax.ShapeDtypeStruct(block, jnp.float32)...  30.9 us
    pallas_call x1, Pallas kernels, adp_gather(): pl.pallas_call(kernel, out_shape=jax.ShapeDtypeStruct((holders,) + own.sh...  15.6 us
    dot_general x2, matrix products, local(): jnp.dot(low_spread, factors[side], preferred_element_type=jnp.float32)  7.17 us
    dot_general x1, matrix products, local(): jnp.dot(hidden, down_weight, preferred_element_type=jnp.float32)  5.52 us
    dot_general x2, matrix products, local(): lax.dot_general(all_rows, gate_up_weight[side], contract_minor, preferred...  4.7 us
    dot_general x1, matrix products, local(): jnp.dot(low_spread, down_out, preferred_element_type=jnp.float32)  4.07 us
    slice x1, local copies, waits for them, and re-layouts, local(): all_rows = gathered[:, :tok_rows, :width].reshape(-1, width)  3.96 us

profile of v2, /device:TPU:26, one launch (start us, length us, event | category | flops | bytes accessed | tf_op | source)
XLA Modules:
  0.0 150.6 jit_solution(9957530349310610264)
XLA Ops:
  0.0 0.0 copy-start
  0.0 0.8 fusion.32
  0.9 0.9 select_reduce_fusion
  1.7 1.0 fusion.28
  2.8 0.9 constant_dynamic-slice_fusion
  3.7 0.9 constant_dynamic-slice_fusion.1
  4.6 0.6 pad_maximum_fusion.2.refs_0_
  5.2 0.1 copy.19
  5.3 0.1 reduce-window.8
  5.4 0.1 add_reduce_fusion
  5.5 0.1 select_reduce_fusion.2
  5.7 0.1 select_reduce_fusion.1
  5.8 0.1 concatenate.24
  5.9 1.0 fusion.30
  6.9 1.5 %pad_maximum_fusion.1.factor_ref = bf16[4,48,144]{2,1,0:T(8,128)(2,1)} fusion(bf16[4,16,144]{2,1,0:T(8,128)(2,1)} %bitcast.63, bf16[4,32,144]{2,1,0:T(8,128)(2,1)} %bitcast.61), kind=kLoop, calls=%fused_computation.48 | loop fusion | flops 110592 | bytes 110592 | tf_op jit(solution)/shard_map/concatenate | solution.py:426
  8.4 15.6 %adp_gather.1 = bf16[16,4,2304]{2,1,0:T(4,128)(2,1)} custom-call(bf16[4,2304]{1,0:T(4,128)(2,1)} %pad_maximum_fusion.2.refs_0_), custom_call_target="tpu_custom_call" | custom-call | tf_op jit(solution)/shard_map/adp_gather/pallas_call | solution.py:85
  24.0 1.0 reshape.120
  25.0 0.2 convolution_convert_fusion
  25.3 0.7 pad_maximum_fusion.own_ref
  26.0 57.2 %rows_gather.1 = (bf16[32,48,1920]{2,1,0:T(8,128)(2,1)}, bf16[16,4,48,144]{3,2,1,0:T(8,128)(2,1)}) custom-call(bf16[48,1920]{1,0:T(8,128)(2,1)} %pad_maximum_fusion.own_ref, bf16[4,48,144]{2,1,0:T(8,128)(2,1)} %pad_maximum_fusion.1.factor_ref), custom_call_target="tpu_custom_call" | custom-call | tf_op jit(solution)/shard_map/rows_gather/pallas_call | solution.py:218
  83.2 2.0 %gather_fusion = bf16[16,48,144]{2,1,0:T(8,128)(2,1)S(1)} fusion(bf16[64,48,144]{2,1,0:T(8,128)(2,1)} %bitcast.60, s32[1024]{0:T(1024)S(1)} %pad_clamp_fusion), kind=kCustom, calls=%fused_computation | custom fusion | bytes 442432 | tf_op jit(solution)/shard_map/jit(_take)/gather | solution.py:434
  85.2 0.1 select_bitcast_fusion
  85.4 1.6 %convert_reduce_fusion = s32[32,32]{1,0:T(8,128)S(1)} fusion(bf16[32,48,1920]{2,1,0:T(8,128)(2,1)} %get-tuple-element.7), kind=kLoop, calls=%fused_computation.25 | loop fusion | flops 1024 | bytes 6144 | tf_op jit(solution)/shard_map/convert_element_type | solution.py:447
  87.0 0.1 reshape.128
  87.1 0.7 copy.21
  87.8 0.7 copy.20
  88.5 1.2 slice.63
  89.6 0.5 copy.29
  90.2 0.9 reshape.125
  91.1 1.5 fusion.39
  92.6 4.0 %slice.54 = bf16[32,32,1536]{2,1,0:T(8,128)(2,1)} slice(bf16[32,48,1920]{2,1,0:T(8,128)(2,1)} %get-tuple-element.7), slice={[0:32], [0:32], [0:1536]} | slice | bytes 6291456 | tf_op jit(solution)/shard_map/slice | solution.py:439
  96.6 3.2 %fusion.6 = f32[1024,144]{0,1:T(8,128)S(1)} fusion(bf16[256,144]{1,0:T(8,128)(2,1)} %bitcast.59, bf16[1024,1536]{1,0:T(8,128)(2,1)} %bitcast.48, bf16[256,1536]{1,0:T(8,128)(2,1)S(1)} %bitcast.56, s32[256]{0:T(256)S(1)} %and_select_fusion, s32[1024]{0:T(1024)S(1)} %reshape.128), kind=kOutput, calls=%fused_computation.14 | convolution fusion | flops 881590272 | bytes 4600832 | tf_op jit(solution)/shard_map/dot_general | solution.py:459
  99.8 4.0 %fusion.7 = f32[1024,144]{0,1:T(8,128)} fusion(bf16[256,144]{1,0:T(8,128)(2,1)} %bitcast.58, bf16[1024,1536]{1,0:T(8,128)(2,1)} %bitcast.49, bf16[256,1536]{1,0:T(8,128)(2,1)S(1)} %bitcast.55, s32[256]{0:T(256)S(1)} %and_select_fusion, s32[1024]{0:T(1024)S(1)} %reshape.128), kind=kOutput, calls=%fused_computation.15 | convolution fusion | flops 881590272 | bytes 4600832 | tf_op jit(solution)/shard_map/dot_general | solution.py:459
  103.8 0.0 copy-start.1
  103.8 0.0 copy-start.3
  103.8 3.5 %fusion.14 = f32[1024,144]{0,1:T(8,128)S(1)} fusion(f32[1024,144]{0,1:T(8,128)} %fusion.7, bf16[1024,1536]{1,0:T(8,128)(2,1)} %bitcast.50, bf16[2,144,1536]{2,1,0:T(8,128)(2,1)} %param.12), kind=kOutput, calls=%fused_computation.24 | convolution fusion | flops 454311936 | bytes 4767744 | tf_op jit(solution)/shard_map/dot_general | solution.py:455
  107.3 0.0 copy-done.1
  107.3 0.0 copy-done.3
  107.3 1.2 fusion.5
  108.5 4.1 %fusion.4 = f32[1024,1536]{1,0:T(8,128)} fusion(bf16[256,1536]{1,0:T(8,128)(2,1)S(1)} %reshape.125, bf16[1024,144]{0,1:T(8,128)(2,1)S(1)} %fusion.5, bf16[256,144]{1,0:T(8,128)(2,1)S(1)} %bitcast.57, s32[256]{0:T(256)S(1)} %and_select_fusion, s32[1024]{0:T(1024)S(1)} %reshape.128), kind=kOutput, calls=%fused_computation.12 | convolution fusion | flops 881590272 | bytes 7451648 | tf_op jit(solution)/shard_map/dot_general | solution.py:465
  112.6 0.0 copy-done
  112.6 5.5 %add_convert_fusion = bf16[1024,1536]{1,0:T(8,128)(2,1)} fusion(f32[1024,1536]{1,0:T(8,128)} %fusion.4, bf16[1024,144]{0,1:T(8,128)(2,1)S(1)} %fusion.5, bf16[144,1536]{1,0:T(8,128)(2,1)S(1)} %copy-done), kind=kOutput, calls=%fused_computation.1 | convolution fusion | flops 456130560 | bytes 10174464 | tf_op jit(solution)/shard_map/dot_general | solution.py:465
  118.1 0.0 copy-start.2
  118.1 30.9 %sum_scatter.1 = f32[32,1536]{1,0:T(8,128)} custom-call(bf16[32,32,1536]{2,1,0:T(8,128)(2,1)} %bitcast.52), custom_call_target="tpu_custom_call" | custom-call | tf_op jit(solution)/shard_map/sum_scatter/pallas_call | solution.py:342
  149.0 0.0 copy-done.2
  149.1 1.6 %fusion.31 = bf16[32,1536]{1,0:T(8,128)(2,1)} fusion(f32[32,1536]{1,0:T(8,128)} %sum_scatter.1, bf16[32,1536]{1,0:T(8,128)(2,1)S(1)} %copy-done.2), kind=kLoop, calls=%fused_computation.46 | loop fusion | flops 147456 | bytes 393216 | tf_op jit(solution)/shard_map/convert_element_type | solution.py:469
  (14 shorter events, 0.1 us)
Async XLA Ops:
  0.0 112.6 %copy-start = (bf16[144,1536]{1,0:T(8,128)(2,1)S(1)}, bf16[144,1536]{1,0:T(8,128)(2,1)}, u32[]{:S(2)}) copy-start(bf16[144,1536]{1,0:T(8,128)(2,1)} %param.13) | copy-start | bytes 1327108
  103.8 3.5 %copy-start.1 = (bf16[32,32,1536]{2,1,0:T(8,128)(2,1)S(1)}, bf16[32,32,1536]{2,1,0:T(8,128)(2,1)}, u32[]{:S(2)}) copy-start(bf16[32,32,1536]{2,1,0:T(8,128)(2,1)} %slice.54) | copy-start | bytes 9437188
  103.8 3.5 %copy-start.3 = (bf16[2,144,1536]{2,1,0:T(8,128)(2,1)S(1)}, bf16[2,144,1536]{2,1,0:T(8,128)(2,1)}, u32[]{:S(2)}) copy-start(bf16[2,144,1536]{2,1,0:T(8,128)(2,1)} %param.12) | copy-start | bytes 2654212
  118.1 31.0 %copy-start.2 = (bf16[32,1536]{1,0:T(8,128)(2,1)S(1)}, bf16[32,1536]{1,0:T(8,128)(2,1)}, u32[]{:S(2)}) copy-start(bf16[32,1536]{1,0:T(8,128)(2,1)} %param.10) | copy-start | bytes 294916

commit v3 on v2

--- a/solution.py
+++ b/solution.py
@@ -117,6 +117,8 @@
         sib_recv,
         adp_send,
         adp_recv,
+        adp_across_send,
+        adp_across_recv,
         local_sem,
     ):
         me = lax.axis_index("blk")
@@ -130,8 +132,36 @@
             FWD: {"blk": blk_index(x_hi, lax.rem(z + 1, RING), core)},
             BWD: {"blk": blk_index(x_hi, lax.rem(z + RING - 1, RING), core)},
         }
-        greet([sibling, across, ahead[FWD], ahead[BWD]] + adp_peers(holders))
+        x_lo = lax.rem(me_adp, 2)
+        y = me_adp // 2
+        adp_across = {"adp": y * 2 + 1 - x_lo}
+        adp_ahead = {
+            FWD: {"adp": lax.rem(y + 1, RING) * 2 + x_lo},
+            BWD: {"adp": lax.rem(y + RING - 1, RING) * 2 + x_lo},
+        }
+        greet(
+            [sibling, across, ahead[FWD], ahead[BWD], adp_across, adp_ahead[FWD], adp_ahead[BWD]]
+        )
         sent = []
+
+        def adp_at(stream, way, far):
+            x_of = x_lo if stream == OWN else 1 - x_lo
+            y_of = lax.rem(y + RING - far, RING) if way == FWD else lax.rem(y + far, RING)
+            return y_of * 2 + x_of
+
+        def adp_push(src, index, send_sem, recv_sem, target):
+            copy = remote(src, factor_all_ref.at[index], send_sem, recv_sem, target)
+            copy.start()
+            sent.append(copy)
+
+        def adp_ring(src, index, stream, way, far):
+            adp_push(
+                src,
+                index,
+                adp_send.at[stream, way, far],
+                adp_recv.at[stream, way, far],
+                adp_ahead[way],
+            )
 
         def at(stream, way, far, owner_core):
             x_of = x_hi if stream == OWN else 1 - x_hi
@@ -165,7 +195,9 @@
         to_ring(own_ref, me, OWN, FWD, 0)
         to_ring(own_ref, me, OWN, BWD, 0)
         to_sibling(own_ref, me, OWN, FWD, 0)
-        adp_copies = adp_start(holders, factor_ref, factor_all_ref, adp_send, adp_recv)
+        adp_push(factor_ref, me_adp, adp_across_send, adp_across_recv, adp_across)
+        adp_ring(factor_ref, me_adp, OWN, FWD, 0)
+        adp_ring(factor_ref, me_adp, OWN, BWD, 0)
         keep = pltpu.make_async_copy(own_ref, all_ref.at[me], local_sem.at[0])
         keep.start()
         keep_factor = pltpu.make_async_copy(factor_ref, factor_all_ref.at[me_adp], local_sem.at[1])
@@ -177,6 +209,11 @@
         to_ring(slab, other, OTHER, FWD, 0)
         to_ring(slab, other, OTHER, BWD, 0)
         to_sibling(slab, other, OTHER, FWD, 0)
+        adp_other = adp_at(OTHER, FWD, 0)
+        slab = factor_all_ref.at[adp_other]
+        remote(slab, slab, adp_across_send, adp_across_recv, adp_across).wait_recv()
+        adp_ring(slab, adp_other, OTHER, FWD, 0)
+        adp_ring(slab, adp_other, OTHER, BWD, 0)
         for far in range(1, 5):
             for stream in (OWN, OTHER):
                 for way in (FWD, BWD):
@@ -195,6 +232,17 @@
                     if far < last:
                         to_ring(slab, index, stream, way, far)
                     to_sibling(slab, index, stream, way, far)
+                    index = adp_at(stream, way, far)
+                    slab = factor_all_ref.at[index]
+                    remote(
+                        slab,
+                        slab,
+                        adp_send.at[stream, way, far - 1],
+                        adp_recv.at[stream, way, far - 1],
+                        adp_ahead[way],
+                    ).wait_recv()
+                    if far < last:
+                        adp_ring(slab, index, stream, way, far)
         for far in range(0, 5):
             for stream in (OWN, OTHER):
                 for way in (FWD, BWD):
@@ -208,7 +256,6 @@
                         sib_recv.at[stream, way, far],
                         sibling,
                     ).wait_recv()
-        adp_finish(holders, adp_copies, factor_all_ref, adp_recv, adp_send)
         for copy in sent:
             copy.wait_send()
         keep.wait()
@@ -230,8 +277,10 @@
             dma,
             dma((2, 2, 5)),
             dma((2, 2, 5)),
-            dma((holders - 1,)),
-            dma((holders - 1,)),
+            dma((2, 2, 4)),
+            dma((2, 2, 4)),
+            dma,
+            dma,
             dma((2,)),
         ],
         compiler_params=pltpu.CompilerParams(collective_id=2, has_side_effects=True),
@@ -239,12 +288,25 @@
     )(own, factors)
 
 
-def sum_scatter(parts):
-    rows, width = parts.shape[1:]
+def block_scatter(gathered, gate_up, factors, down, stream_rows):
+    rows, width = stream_rows.shape
+    rank_pairs = gathered.shape[0]
+    cat_rows = factors.shape[1]
+    kind = gathered.dtype
+    piece = width // 6
+    minor = (((1,), (1,)), ((), ()))
 
     def kernel(
+        all_ref,
+        gate_up_ref,
+        factor_ref,
+        down_ref,
+        stream_ref,
+        out_ref,
+        group_ref,
+        rows_in_ref,
+        down_out_ref,
         part_ref,
-        out_ref,
         sib_ref,
         leave_ref,
         arrive_ref,
@@ -279,28 +341,83 @@
             copy.start()
             sent.append(copy)
 
-        order = []
-        for far in range(4, -1, -1):
-            for stream in (OTHER, OWN):
-                for way in (FWD, BWD):
-                    if far <= reach(stream, way) and not (far == 0 and way == BWD):
-                        order.append((stream, way, far))
+        def keys_at(far):
+            return [
+                (stream, way, far)
+                for stream in (OTHER, OWN)
+                for way in (FWD, BWD)
+                if far <= reach(stream, way) and not (far == 0 and way == BWD)
+            ]
 
         def sib_copy(stream, way, far):
             return remote(
-                part_ref.at[at(stream, way, far, 1 - core)],
+                part_ref.at[1, stream, way, far],
                 sib_ref.at[stream, way, far],
                 sib_send.at[stream, way, far],
                 sib_recv.at[stream, way, far],
                 sibling,
             )
 
-        for key in order:
-            push(sib_copy(*key))
+        for k in range(rank_pairs):
+            rows_in_ref[k * ACTIVE : (k + 1) * ACTIVE, :] = all_ref[
+                k, rows : rows + ACTIVE, :width
+            ]
+            rank, side = k // 2, k % 2
+            for p in range(3):
+                start = (side * 3 + p) * piece
+                down_out_ref[rank * ACTIVE : (rank + 1) * ACTIVE, start : start + piece] = all_ref[
+                    k, p * ACTIVE : (p + 1) * ACTIVE, width : width + piece
+                ]
+
+        def compute(far):
+            keys = keys_at(far)
+            slots = [(side,) + key for side in (1, 0) for key in keys]
+            count = len(slots) * rows
+            numbers = []
+            for place, (side, stream, way, _) in enumerate(slots):
+                index = at(stream, way, far, core if side == 0 else 1 - core)
+                group_ref[place * rows : (place + 1) * rows, :] = all_ref[index, :rows, :width]
+                numbers.append(all_ref[index, :rows, width + piece :].astype(jnp.float32))
+            number = jnp.concatenate(numbers, axis=0)
+            number = jnp.concatenate([number] * (cat_rows // number.shape[1]), axis=1)
+            lane = lax.broadcasted_iota(jnp.int32, (count, cat_rows), 1)
+            match = number == lax.rem(lane, ACTIVE).astype(jnp.float32)
+
+            def spread(low):
+                return jnp.where(match, low, 0.0).astype(kind)
+
+            group = group_ref[:count, :]
+            pre = []
+            for side in range(2):
+                low = lax.dot_general(
+                    group,
+                    rows_in_ref[side * cat_rows : (side + 1) * cat_rows, :],
+                    minor,
+                    preferred_element_type=jnp.float32,
+                )
+                base = lax.dot_general(
+                    group, gate_up_ref[side], minor, preferred_element_type=jnp.float32
+                )
+                pre.append(
+                    base
+                    + jnp.dot(spread(low), factor_ref[side], preferred_element_type=jnp.float32)
+                )
+            hidden = (jax.nn.gelu(pre[0], approximate=True) * pre[1]).astype(kind)
+            low = lax.dot_general(
+                hidden, factor_ref[2], minor, preferred_element_type=jnp.float32
+            )
+            part = jnp.dot(hidden, down_ref[...], preferred_element_type=jnp.float32) + jnp.dot(
+                spread(low), down_out_ref[...], preferred_element_type=jnp.float32
+            )
+            part = part.astype(kind)
+            for place, slot in enumerate(slots):
+                part_ref[slot] = part[place * rows : (place + 1) * rows, :]
+            for key in keys:
+                push(sib_copy(*key))
 
         def pair_sum(stream, way, far):
             sib_copy(stream, way, far).wait_recv()
-            own = part_ref[at(stream, way, far, core)].astype(jnp.float32)
+            own = part_ref[0, stream, way, far].astype(jnp.float32)
             return own + sib_ref[stream, way, far].astype(jnp.float32)
 
         def ring_copy(stream, way, far):
@@ -317,23 +434,31 @@
             return arrive_ref[stream, way, far].astype(jnp.float32)
 
         totals = {}
-        for key in order:
-            stream, way, far = key
-            total = pair_sum(*key)
-            if far == 0:
-                total = total + arrived(stream, FWD, 0) + arrived(stream, BWD, 0)
-                if stream == OTHER:
-                    cross_out_ref[...] = total.astype(cross_out_ref.dtype)
-                    push(remote(cross_out_ref, cross_in_ref, across_send, across_recv, across))
-                else:
-                    totals[stream] = total
-                continue
-            if far < reach(stream, way):
-                total = total + arrived(stream, way, far)
-            leave_ref[stream, way, far - 1] = total.astype(leave_ref.dtype)
-            push(ring_copy(stream, way, far))
+
+        def pass_on(far):
+            for stream, way, _ in keys_at(far):
+                total = pair_sum(stream, way, far)
+                if far == 0:
+                    total = total + arrived(stream, FWD, 0) + arrived(stream, BWD, 0)
+                    if stream == OTHER:
+                        cross_out_ref[...] = total.astype(kind)
+                        push(remote(cross_out_ref, cross_in_ref, across_send, across_recv, across))
+                    else:
+                        totals[stream] = total
+                    continue
+                if far < reach(stream, way):
+                    total = total + arrived(stream, way, far)
+                leave_ref[stream, way, far - 1] = total.astype(kind)
+                push(ring_copy(stream, way, far))
+
+        compute(4)
+        for far in range(3, -1, -1):
+            compute(far)
+            pass_on(far + 1)
+        pass_on(0)
         remote(cross_out_ref, cross_in_ref, across_send, across_recv, across).wait_recv()
-        out_ref[...] = totals[OWN] + cross_in_ref[...].astype(jnp.float32)
+        total = totals[OWN] + cross_in_ref[...].astype(jnp.float32)
+        out_ref[...] = (stream_ref[...].astype(jnp.float32) + total).astype(kind)
         for copy in sent:
             copy.wait_send()
 
@@ -341,15 +466,19 @@
     block = (rows, width)
     return pl.pallas_call(
         kernel,
-        out_shape=jax.ShapeDtypeStruct(block, jnp.float32),
-        in_specs=[pl.BlockSpec(memory_space=pltpu.VMEM)],
+        out_shape=jax.ShapeDtypeStruct(block, kind),
+        in_specs=[pl.BlockSpec(memory_space=pltpu.VMEM)] * 5,
         out_specs=pl.BlockSpec(memory_space=pltpu.VMEM),
         scratch_shapes=[
-            pltpu.VMEM((2, 2, 5) + block, parts.dtype),
-            pltpu.VMEM((2, 2, 4) + block, parts.dtype),
-            pltpu.VMEM((2, 2, 4) + block, parts.dtype),
-            pltpu.VMEM(block, parts.dtype),
-            pltpu.VMEM(block, parts.dtype),
+            pltpu.VMEM((8 * rows, width), kind),
+            pltpu.VMEM((2 * cat_rows, width), kind),
+            pltpu.VMEM((cat_rows, width), kind),
+            pltpu.VMEM((2, 2, 2, 5) + block, kind),
+            pltpu.VMEM((2, 2, 5) + block, kind),
+            pltpu.VMEM((2, 2, 4) + block, kind),
+            pltpu.VMEM((2, 2, 4) + block, kind),
+            pltpu.VMEM(block, kind),
+            pltpu.VMEM(block, kind),
             dma((2, 2, 4)),
             dma((2, 2, 4)),
             dma,
@@ -358,8 +487,8 @@
             dma((2, 2, 5)),
         ],
         compiler_params=pltpu.CompilerParams(collective_id=3, has_side_effects=True),
-        name="sum_scatter",
-    )(parts)
+        name="block_scatter",
+    )(gathered, gate_up, factors, down, stream_rows)
 
 
 def local(
@@ -436,37 +565,7 @@
     ).transpose(1, 0, 2)
     cat_rows = ACTIVE * rank_columns
     factors = factors.reshape(3, cat_rows, hidden_dev)
-    all_rows = gathered[:, :tok_rows, :width].reshape(-1, width)
-    rows_in = gathered[:, tok_rows:, :width].reshape(2, cat_rows, width)
-    down_out = (
-        gathered[:, :, width : width + tile_cols]
-        .reshape(rank_columns, 2, 3, ACTIVE, tile_cols)
-        .transpose(0, 3, 1, 2, 4)
-        .reshape(cat_rows, width)
-    )
-    all_slot = gathered[:, :tok_rows, width + tile_cols].reshape(-1, 1).astype(jnp.int32)
-    match = all_slot == (jnp.arange(cat_rows, dtype=jnp.int32) % ACTIVE)[None, :]
-    contract_minor = (((1,), (1,)), ((), ()))
-    pre = []
-    for side in range(2):
-        low = lax.dot_general(
-            all_rows, rows_in[side], contract_minor, preferred_element_type=jnp.float32
-        )
-        base = lax.dot_general(
-            all_rows, gate_up_weight[side], contract_minor, preferred_element_type=jnp.float32
-        )
-        low_spread = jnp.where(match, low, 0).astype(jnp.bfloat16)
-        pre.append(base + jnp.dot(low_spread, factors[side], preferred_element_type=jnp.float32))
-    hidden = (jax.nn.gelu(pre[0], approximate=True) * pre[1]).astype(jnp.bfloat16)
-    low_part = lax.dot_general(
-        hidden, factors[2], contract_minor, preferred_element_type=jnp.float32
-    )
-    low_spread = jnp.where(match, low_part, 0).astype(jnp.bfloat16)
-    part = jnp.dot(hidden, down_weight, preferred_element_type=jnp.float32) + jnp.dot(
-        low_spread, down_out, preferred_element_type=jnp.float32
-    )
-    total = sum_scatter(part.astype(jnp.bfloat16).reshape(-1, tok_rows, width))
-    return (stream.astype(jnp.float32) + total).astype(jnp.bfloat16)
+    return block_scatter(gathered, gate_up_weight, factors, down_weight, stream)
 
 
 def solution(mesh):

time: 151 us -> 115 us (0.76)
  the two profiles are of different devices: /device:TPU:26 before, /device:TPU:6 now
where the time goes in v3:
time: 115 us; the launch traced here: 114 us
  Pallas kernels  99.7 us (87%)
  other arithmetic  7.08 us (6%)
  local copies, waits for them, and re-layouts  6.56 us (6%)
    pallas_call x1, Pallas kernels, rows_gather(): pl.pallas_call(kernel, out_shape=[jax.ShapeDtypeStruct((blocks,) + own.sh...  47.7 us
    pallas_call x1, Pallas kernels, block_scatter(): pl.pallas_call(kernel, out_shape=jax.ShapeDtypeStruct(block, kind), in_sp...  35.3 us
    pallas_call x1, Pallas kernels, adp_gather(): pl.pallas_call(kernel, out_shape=jax.ShapeDtypeStruct((holders,) + own.sh...  16.6 us

profile of v3, /device:TPU:6, one launch (start us, length us, event | category | flops | bytes accessed | tf_op | source)
XLA Modules:
  0.0 113.7 jit_solution(16786100775315259297)
XLA Ops:
  0.0 0.0 copy-start
  0.0 0.8 fusion.3
  0.9 0.9 select_reduce_fusion
  1.7 1.0 fusion
  2.8 0.9 constant_dynamic-slice_fusion
  3.7 0.0 copy-done
  3.7 0.6 pad_maximum_fusion.2.refs_0_
  4.4 0.1 copy.14
  4.5 0.1 reduce-window.8
  4.5 0.1 add_reduce_fusion
  4.7 0.1 select_reduce_fusion.2
  4.8 0.1 select_reduce_fusion.1
  4.9 0.1 concatenate.24
  5.0 1.0 fusion.2
  6.0 1.5 %pad_maximum_fusion.1.factor_ref = bf16[4,48,144]{2,1,0:T(8,128)(2,1)} fusion(bf16[4,16,144]{2,1,0:T(8,128)(2,1)} %bitcast.23, bf16[4,32,144]{2,1,0:T(8,128)(2,1)} %bitcast.21), kind=kLoop, calls=%fused_computation.9 | loop fusion | flops 110592 | bytes 110592 | tf_op jit(solution)/shard_map/concatenate | solution.py:555
  7.5 16.6 %adp_gather.1 = bf16[16,4,2304]{2,1,0:T(4,128)(2,1)} custom-call(bf16[4,2304]{1,0:T(4,128)(2,1)} %pad_maximum_fusion.2.refs_0_), custom_call_target="tpu_custom_call" | custom-call | tf_op jit(solution)/shard_map/adp_gather/pallas_call | solution.py:85
  24.1 1.0 reshape.81
  25.2 0.2 convolution_convert_fusion
  25.4 0.7 pad_maximum_fusion.own_ref
  26.1 47.7 %rows_gather.1 = (bf16[32,48,1920]{2,1,0:T(8,128)(2,1)}, bf16[16,4,48,144]{3,2,1,0:T(8,128)(2,1)}) custom-call(bf16[48,1920]{1,0:T(8,128)(2,1)} %pad_maximum_fusion.own_ref, bf16[4,48,144]{2,1,0:T(8,128)(2,1)} %pad_maximum_fusion.1.factor_ref), custom_call_target="tpu_custom_call" | custom-call | tf_op jit(solution)/shard_map/rows_gather/pallas_call | solution.py:265
  73.8 2.0 %gather_fusion = bf16[16,48,144]{2,1,0:T(8,128)(2,1)S(1)} fusion(bf16[64,48,144]{2,1,0:T(8,128)(2,1)} %bitcast.20, s32[1024]{0:T(1024)S(1)} %pad_clamp_fusion), kind=kCustom, calls=%fused_computation | custom fusion | bytes 442432 | tf_op jit(solution)/shard_map/jit(_take)/gather | solution.py:563
  75.8 0.1 select_bitcast_fusion
  75.9 0.9 copy.15
  76.8 35.3 %block_scatter.1 = bf16[32,1536]{1,0:T(8,128)(2,1)} custom-call(bf16[32,48,1920]{2,1,0:T(8,128)(2,1)} %get-tuple-element.7.all_ref, bf16[2,144,1536]{2,1,0:T(8,128)(2,1)} %gate_up_ref.1, bf16[3,256,144]{2,1,0:T(8,128)(2,1)} %bitcast.19, bf16[144,1536]{1,0:T(8,128)(2,1)} %down_ref.1, bf16[32,1536]{1,0:T(8,128)(2,1)} %stream_ref.1), custom_call_target="tpu_custom_call" | custom-call | tf_op jit(solution)/shard_map/block_scatter/pallas_call | solution.py:467
  112.2 1.5 %copy.23 = bf16[32,1536]{1,0:T(8,128)(2,1)} copy(bf16[32,1536]{1,0:T(8,128)(2,1)} %block_scatter.1) | data formatting | bytes 196608
  (12 shorter events, 0.1 us)
Async XLA Ops:
  0.0 3.7 %copy-start = (bf16[4,32,1536]{2,1,0:T(8,128)(2,1)S(1)}, bf16[4,32,1536]{2,1,0:T(8,128)(2,1)}, u32[]{:S(2)}) copy-start(bf16[4,32,1536]{2,1,0:T(8,128)(2,1)} %param.14) | copy-start | bytes 1179652

commit v4 on v3

v4 whole, which is shorter than its diff:
```python
import jax
import jax.numpy as jnp
from jax import lax
from jax.experimental import pallas as pl
from jax.experimental.pallas import tpu as pltpu
from jax.sharding import PartitionSpec as P

ACTIVE = 16
RING = 8
FWD, BWD = 0, 1
OWN, OTHER = 0, 1

norm_eps = 1e-06


def normalize(rows, gain):
    value_rows = rows.astype(jnp.float32)
    scale = lax.rsqrt(jnp.mean(value_rows * value_rows, axis=-1, keepdims=True) + norm_eps)
    return (value_rows * scale * gain).astype(jnp.bfloat16)


def blk_index(x_hi, z, core):
    return x_hi * (2 * RING) + z * 2 + core


def greet(targets):
    barrier = pltpu.get_barrier_semaphore()
    for target in targets:
        pl.semaphore_signal(
            barrier, inc=1, device_id=target, device_id_type=pl.DeviceIdType.MESH
        )
    pl.semaphore_wait(barrier, len(targets))


def remote(src, dst, send_sem, recv_sem, target):
    return pltpu.make_async_remote_copy(
        src_ref=src,
        dst_ref=dst,
        send_sem=send_sem,
        recv_sem=recv_sem,
        device_id=target,
        device_id_type=pl.DeviceIdType.MESH,
    )


def reach(stream, way):
    return 4 if (stream == OWN) == (way == FWD) else 3


ROWS, PICKS, FACTORS = 0, 1, 2


def rows_gather(own, catalog_rows, choose, factors, holders):
    blocks = 4 * RING
    kept, catalog_width = catalog_rows.shape
    chunk = catalog_width // 6
    picks = choose.shape[1]

    def kernel(
        own_ref,
        catalog_own_ref,
        choose_ref,
        factor_ref,
        all_ref,
        picks_all_ref,
        factor_all_ref,
        catalog_ref,
        picks_ref,
        ring_send,
        ring_recv,
        across_send,
        across_recv,
        sib_send,
        sib_recv,
        catalog_send,
        catalog_recv,
        local_sem,
    ):
        me = lax.axis_index("blk")
        me_adp = lax.axis_index("adp")
        x_hi = me // (2 * RING)
        z = lax.rem(me // 2, RING)
        core = lax.rem(me, 2)
        x_lo = lax.rem(me_adp, 2)
        y = me_adp // 2
        sibling = {"blk": blk_index(x_hi, z, 1 - core)}
        blk_across = {"blk": blk_index(1 - x_hi, z, core)}
        blk_ahead = {
            FWD: {"blk": blk_index(x_hi, lax.rem(z + 1, RING), core)},
            BWD: {"blk": blk_index(x_hi, lax.rem(z + RING - 1, RING), core)},
        }
        adp_across = {"adp": y * 2 + 1 - x_lo}
        adp_ahead = {
            FWD: {"adp": lax.rem(y + 1, RING) * 2 + x_lo},
            BWD: {"adp": lax.rem(y + RING - 1, RING) * 2 + x_lo},
        }
        adp_peers = [{"adp": lax.rem(me_adp + step, holders)} for step in range(1, holders)]
        across = [blk_across, blk_across, adp_across]
        ahead = [blk_ahead, blk_ahead, adp_ahead]
        source = [own_ref, picks_ref, factor_ref]
        landing = [all_ref, picks_all_ref, factor_all_ref]
        greet([sibling, blk_across, blk_ahead[FWD], blk_ahead[BWD]] + adp_peers)
        sent = []

        def around(at, way, far):
            return lax.rem(at + RING - far, RING) if way == FWD else lax.rem(at + far, RING)

        def index_of(kind, stream, way, far, owner_core):
            if kind == FACTORS:
                return around(y, way, far) * 2 + (x_lo if stream == OWN else 1 - x_lo)
            x_of = x_hi if stream == OWN else 1 - x_hi
            return blk_index(x_of, around(z, way, far), owner_core)

        def push(copy):
            copy.start()
            sent.append(copy)

        def to_ring(src, index, kind, stream, way, far):
            push(
                remote(
                    src,
                    landing[kind].at[index],
                    ring_send.at[kind, stream, way, far],
                    ring_recv.at[kind, stream, way, far],
                    ahead[kind][way],
                )
            )

        def to_sibling(src, index, kind, stream, way, far):
            if kind == FACTORS:
                return
            push(
                remote(
                    src,
                    landing[kind].at[index],
                    sib_send.at[kind, stream, way, far],
                    sib_recv.at[kind, stream, way, far],
                    sibling,
                )
            )

        def launch(kind):
            index = index_of(kind, OWN, FWD, 0, core)
            src = source[kind]
            push(
                remote(
                    src,
                    landing[kind].at[index],
                    across_send.at[kind],
                    across_recv.at[kind],
                    across[kind],
                )
            )
            to_ring(src, index, kind, OWN, FWD, 0)
            to_ring(src, index, kind, OWN, BWD, 0)
            to_sibling(src, index, kind, OWN, FWD, 0)
            keep = pltpu.make_async_copy(src, landing[kind].at[index], local_sem.at[kind])
            keep.start()
            return keep

        def join(kind):
            index = index_of(kind, OTHER, FWD, 0, core)
            slab = landing[kind].at[index]
            remote(
                slab, slab, across_send.at[kind], across_recv.at[kind], across[kind]
            ).wait_recv()
            to_ring(slab, index, kind, OTHER, FWD, 0)
            to_ring(slab, index, kind, OTHER, BWD, 0)
            to_sibling(slab, index, kind, OTHER, FWD, 0)

        def relay(kind, stream, far):
            for way in (FWD, BWD):
                last = reach(stream, way)
                if far > last:
                    continue
                index = index_of(kind, stream, way, far, core)
                slab = landing[kind].at[index]
                remote(
                    slab,
                    slab,
                    ring_send.at[kind, stream, way, far - 1],
                    ring_recv.at[kind, stream, way, far - 1],
                    ahead[kind][way],
                ).wait_recv()
                if far < last:
                    to_ring(slab, index, kind, stream, way, far)
                to_sibling(slab, index, kind, stream, way, far)

        keeps = [launch(ROWS)]
        for step, target in enumerate(adp_peers):
            copy = remote(
                catalog_own_ref,
                catalog_ref.at[me_adp],
                catalog_send.at[step],
                catalog_recv.at[step],
                target,
            )
            push(copy)
        keep = pltpu.make_async_copy(catalog_own_ref, catalog_ref.at[me_adp], local_sem.at[3])
        keep.start()
        keeps.append(launch(FACTORS))
        relay(ROWS, OWN, 1)
        join(ROWS)
        relay(ROWS, OWN, 2)

        for step, target in enumerate(adp_peers):
            slab = catalog_ref.at[lax.rem(me_adp + holders - step - 1, holders)]
            remote(
                slab, slab, catalog_send.at[step], catalog_recv.at[step], target
            ).wait_recv()
        keep.wait()
        for part in range(6):
            cols = slice(part * chunk, (part + 1) * chunk)
            total = jnp.zeros((picks, chunk), jnp.float32)
            for holder in range(holders):
                held = catalog_ref[holder, :, cols].astype(jnp.float32)
                for row in range(kept):
                    mask = jnp.concatenate([choose_ref[holder * kept + row]] * (chunk // 128), axis=1)
                    total = total + mask * held[row : row + 1, :]
            picks_ref[:, cols] = total.astype(picks_ref.dtype)

        keeps.append(launch(PICKS))
        relay(ROWS, OTHER, 1)
        join(FACTORS)
        relay(FACTORS, OWN, 1)
        relay(ROWS, OWN, 3)
        relay(ROWS, OTHER, 2)
        relay(PICKS, OWN, 1)
        join(PICKS)
        relay(FACTORS, OTHER, 1)
        relay(FACTORS, OWN, 2)
        relay(ROWS, OTHER, 3)
        relay(ROWS, OWN, 4)
        relay(PICKS, OWN, 2)
        relay(PICKS, OTHER, 1)
        relay(FACTORS, OTHER, 2)
        relay(FACTORS, OWN, 3)
        relay(ROWS, OTHER, 4)
        relay(PICKS, OWN, 3)
        relay(PICKS, OTHER, 2)
        relay(FACTORS, OTHER, 3)
        relay(FACTORS, OWN, 4)
        relay(PICKS, OTHER, 3)
        relay(PICKS, OWN, 4)
        relay(FACTORS, OTHER, 4)
        relay(PICKS, OTHER, 4)
        for kind in (ROWS, PICKS):
            for far in range(0, 5):
                for stream in (OWN, OTHER):
                    for way in (FWD, BWD):
                        if far > reach(stream, way) or (far == 0 and way == BWD):
                            continue
                        slab = landing[kind].at[index_of(kind, stream, way, far, 1 - core)]
                        remote(
                            slab,
                            slab,
                            sib_send.at[kind, stream, way, far],
                            sib_recv.at[kind, stream, way, far],
                            sibling,
                        ).wait_recv()
        for copy in sent:
            copy.wait_send()
        for keep in keeps:
            keep.wait()

    dma = pltpu.SemaphoreType.DMA
    return pl.pallas_call(
        kernel,
        out_shape=[
            jax.ShapeDtypeStruct((blocks,) + own.shape, own.dtype),
            jax.ShapeDtypeStruct((blocks, picks, catalog_width), own.dtype),
            jax.ShapeDtypeStruct((holders,) + factors.shape, factors.dtype),
        ],
        in_specs=[pl.BlockSpec(memory_space=pltpu.VMEM)] * 4,
        out_specs=[pl.BlockSpec(memory_space=pltpu.VMEM)] * 3,
        scratch_shapes=[
            pltpu.VMEM((holders, kept, catalog_width), own.dtype),
            pltpu.VMEM((picks, catalog_width), own.dtype),
            dma((3, 2, 2, 4)),
            dma((3, 2, 2, 4)),
            dma((3,)),
            dma((3,)),
            dma((2, 2, 2, 5)),
            dma((2, 2, 2, 5)),
            dma((holders - 1,)),
            dma((holders - 1,)),
            dma((4,)),
        ],
        compiler_params=pltpu.CompilerParams(collective_id=2, has_side_effects=True),
        name="rows_gather",
    )(own, catalog_rows, choose, factors)


def block_scatter(gathered, picks, gate_up, factors, down, stream_rows):
    rows, width = stream_rows.shape
    rank_pairs = gathered.shape[0]
    cat_rows = factors.shape[1]
    kind = gathered.dtype
    half = width // 2
    minor = (((1,), (1,)), ((), ()))

    def kernel(
        all_ref,
        picks_ref,
        gate_up_ref,
        factor_ref,
        down_ref,
        stream_ref,
        out_ref,
        group_ref,
        rows_in_ref,
        down_out_ref,
        part_ref,
        sib_ref,
        leave_ref,
        arrive_ref,
        cross_out_ref,
        cross_in_ref,
        ring_send,
        ring_recv,
        across_send,
        across_recv,
        sib_send,
        sib_recv,
    ):
        me = lax.axis_index("blk")
        x_hi = me // (2 * RING)
        z = lax.rem(me // 2, RING)
        core = lax.rem(me, 2)
        sibling = {"blk": blk_index(x_hi, z, 1 - core)}
        across = {"blk": blk_index(1 - x_hi, z, core)}
        ahead = {
            FWD: {"blk": blk_index(x_hi, lax.rem(z + 1, RING), core)},
            BWD: {"blk": blk_index(x_hi, lax.rem(z + RING - 1, RING), core)},
        }
        greet([sibling, across, ahead[FWD], ahead[BWD]])
        sent = []

        def at(stream, way, far, owner_core):
            x_of = x_hi if stream == OWN else 1 - x_hi
            z_of = lax.rem(z + far, RING) if way == FWD else lax.rem(z + RING - far, RING)
            return blk_index(x_of, z_of, owner_core)

        def push(copy):
            copy.start()
            sent.append(copy)

        def keys_at(far):
            return [
                (stream, way, far)
                for stream in (OTHER, OWN)
                for way in (FWD, BWD)
                if far <= reach(stream, way) and not (far == 0 and way == BWD)
            ]

        def sib_copy(stream, way, far):
            return remote(
                part_ref.at[1, stream, way, far],
                sib_ref.at[stream, way, far],
                sib_send.at[stream, way, far],
                sib_recv.at[stream, way, far],
                sibling,
            )

        for k in range(rank_pairs):
            rows_in_ref[k * ACTIVE : (k + 1) * ACTIVE, :] = picks_ref[k, :, :width]
            rank, start = k // 2, (k % 2) * half
            down_out_ref[rank * ACTIVE : (rank + 1) * ACTIVE, start : start + half] = picks_ref[
                k, :, width:
            ]

        def compute(far):
            keys = keys_at(far)
            slots = [(side,) + key for side in (1, 0) for key in keys]
            count = len(slots) * rows
            numbers = []
            for place, (side, stream, way, _) in enumerate(slots):
                index = at(stream, way, far, core if side == 0 else 1 - core)
                group_ref[place * rows : (place + 1) * rows, :] = all_ref[index, :, :width]
                numbers.append(all_ref[index, :, width:].astype(jnp.float32))
            number = jnp.concatenate(numbers, axis=0)
            number = jnp.concatenate([number] * (cat_rows // number.shape[1]), axis=1)
            lane = lax.broadcasted_iota(jnp.int32, (count, cat_rows), 1)
            match = number == lax.rem(lane, ACTIVE).astype(jnp.float32)

            def spread(low):
                return jnp.where(match, low, 0.0).astype(kind)

            group = group_ref[:count, :]
            pre = []
            for side in range(2):
                low = lax.dot_general(
                    group,
                    rows_in_ref[side * cat_rows : (side + 1) * cat_rows, :],
                    minor,
                    preferred_element_type=jnp.float32,
                )
                base = lax.dot_general(
                    group, gate_up_ref[side], minor, preferred_element_type=jnp.float32
                )
                pre.append(
                    base
                    + jnp.dot(spread(low), factor_ref[side], preferred_element_type=jnp.float32)
                )
            hidden = (jax.nn.gelu(pre[0], approximate=True) * pre[1]).astype(kind)
            low = lax.dot_general(
                hidden, factor_ref[2], minor, preferred_element_type=jnp.float32
            )
            part = jnp.dot(hidden, down_ref[...], preferred_element_type=jnp.float32) + jnp.dot(
                spread(low), down_out_ref[...], preferred_element_type=jnp.float32
            )
            part = part.astype(kind)
            for place, slot in enumerate(slots):
                part_ref[slot] = part[place * rows : (place + 1) * rows, :]
            for key in keys:
                push(sib_copy(*key))

        def pair_sum(stream, way, far):
            sib_copy(stream, way, far).wait_recv()
            own = part_ref[0, stream, way, far].astype(jnp.float32)
            return own + sib_ref[stream, way, far].astype(jnp.float32)

        def ring_copy(stream, way, far):
            return remote(
                leave_ref.at[stream, way, far - 1],
                arrive_ref.at[stream, way, far - 1],
                ring_send.at[stream, way, far - 1],
                ring_recv.at[stream, way, far - 1],
                ahead[way],
            )

        def arrived(stream, way, far):
            ring_copy(stream, way, far + 1).wait_recv()
            return arrive_ref[stream, way, far].astype(jnp.float32)

        totals = {}

        def pass_on(far):
            for stream, way, _ in keys_at(far):
                total = pair_sum(stream, way, far)
                if far == 0:
                    total = total + arrived(stream, FWD, 0) + arrived(stream, BWD, 0)
                    if stream == OTHER:
                        cross_out_ref[...] = total.astype(kind)
                        push(remote(cross_out_ref, cross_in_ref, across_send, across_recv, across))
                    else:
                        totals[stream] = total
                    continue
                if far < reach(stream, way):
                    total = total + arrived(stream, way, far)
                leave_ref[stream, way, far - 1] = total.astype(kind)
                push(ring_copy(stream, way, far))

        compute(4)
        for far in range(3, -1, -1):
            compute(far)
            pass_on(far + 1)
        pass_on(0)
        remote(cross_out_ref, cross_in_ref, across_send, across_recv, across).wait_recv()
        total = totals[OWN] + cross_in_ref[...].astype(jnp.float32)
        out_ref[...] = (stream_ref[...].astype(jnp.float32) + total).astype(kind)
        for copy in sent:
            copy.wait_send()

    dma = pltpu.SemaphoreType.DMA
    block = (rows, width)
    return pl.pallas_call(
        kernel,
        out_shape=jax.ShapeDtypeStruct(block, kind),
        in_specs=[pl.BlockSpec(memory_space=pltpu.VMEM)] * 6,
        out_specs=pl.BlockSpec(memory_space=pltpu.VMEM),
        scratch_shapes=[
            pltpu.VMEM((8 * rows, width), kind),
            pltpu.VMEM((2 * cat_rows, width), kind),
            pltpu.VMEM((cat_rows, width), kind),
            pltpu.VMEM((2, 2, 2, 5) + block, kind),
            pltpu.VMEM((2, 2, 5) + block, kind),
            pltpu.VMEM((2, 2, 4) + block, kind),
            pltpu.VMEM((2, 2, 4) + block, kind),
            pltpu.VMEM(block, kind),
            pltpu.VMEM(block, kind),
            dma((2, 2, 4)),
            dma((2, 2, 4)),
            dma,
            dma,
            dma((2, 2, 5)),
            dma((2, 2, 5)),
        ],
        compiler_params=pltpu.CompilerParams(collective_id=3, has_side_effects=True),
        name="block_scatter",
    )(gathered, picks, gate_up, factors, down, stream_rows)


def local(
    stream,
    prenorm_gain,
    gate_up_weight,
    down_weight,
    adapter_gate_input,
    adapter_gate_output,
    adapter_down_input,
    adapter_down_output,
    adapter_of_request,
    request_of_slot,
):
    width = stream.shape[1]
    tok_rows = stream.shape[0]
    hidden_dev = down_weight.shape[0]
    rank_columns = adapter_down_output.shape[1]
    holders = lax.axis_size("adp")
    kept_rows = adapter_gate_input.shape[0]
    catalog = jnp.arange(kept_rows * holders, dtype=jnp.int32)
    used = jnp.any(adapter_of_request[:, None] == catalog[None, :], axis=0)
    order = jnp.cumsum(used.astype(jnp.int32)) - 1
    active_pos = jnp.arange(ACTIVE, dtype=jnp.int32)
    picked = used[None, :] & (order[None, :] == active_pos[:, None])
    active = jnp.sum(jnp.where(picked, catalog[None, :], 0), axis=1)
    table = jnp.arange(adapter_of_request.shape[0], dtype=jnp.int32)
    own_adapter = jnp.sum(
        jnp.where(request_of_slot[:, None] == table[None, :], adapter_of_request[None, :], 0),
        axis=1,
    )
    own_match = own_adapter[:, None] == active[None, :]
    own_slot = jnp.sum(jnp.where(own_match, active_pos[None, :], 0), axis=1)
    normed = normalize(stream, prenorm_gain)
    place = lax.axis_index("blk")
    half = width // 2
    row_in = lax.dynamic_slice_in_dim(adapter_gate_input, place, 1, axis=1)[:, 0]
    row_out = lax.dynamic_slice(
        adapter_down_output, (0, place // 2, lax.rem(place, 2) * half), (kept_rows, 1, half)
    )[:, 0]
    catalog_rows = jnp.concatenate([row_in, row_out], axis=1)
    choose = (catalog[:, None] == active[None, :]).astype(jnp.float32)
    choose = jnp.broadcast_to(choose[:, :, None], choose.shape + (128,))
    packed = jnp.concatenate(
        [normed, jnp.broadcast_to(own_slot.astype(jnp.bfloat16)[:, None], (tok_rows, 128))], axis=1
    )
    own_factors = jnp.concatenate(
        [
            adapter_gate_output.reshape(kept_rows, 2 * rank_columns, hidden_dev),
            adapter_down_input.transpose(0, 2, 1),
        ],
        axis=1,
    )
    gathered, picks, factors = rows_gather(packed, catalog_rows, choose, own_factors, holders)
    factors = jnp.take(
        factors.reshape(kept_rows * holders, 3 * rank_columns, hidden_dev), active, axis=0
    ).transpose(1, 0, 2)
    cat_rows = ACTIVE * rank_columns
    factors = factors.reshape(3, cat_rows, hidden_dev)
    return block_scatter(gathered, picks, gate_up_weight, factors, down_weight, stream)


def solution(mesh):
    in_specs = (
        P(("blk", "adp"), None),
        P(),
        P(None, "blk", None),
        P("blk", None),
        P("adp", None, None),
        P("adp", None, None, "blk"),
        P("adp", "blk", None),
        P("adp", None, None),
        P(),
        P(("blk", "adp")),
    )
    out_specs = P(("blk", "adp"), None)
    return jax.shard_map(local, mesh=mesh, in_specs=in_specs, out_specs=out_specs, check_vma=False)
```

time: 115 us -> 106 us (0.922)
  Pallas kernels: 99.7 us -> 91.5 us
    pallas_call x1 -> x0, Pallas kernels: 16.6 us -> none  [adp_gather(): pl.pallas_call(kernel, out_shape=jax.ShapeDtypeStruct((holders,) + own.sh...]
    pallas_call x1, Pallas kernels: 47.7 us -> 56.8 us  [rows_gather(): pl.pallas_call(kernel, out_shape=[jax.ShapeDtypeStruct((blocks,) + own.sh...]
where the time goes in v4:
time: 106 us; the launch traced here: 105 us
  Pallas kernels  91.5 us (86%)
  other arithmetic  7 us (7%)
  local copies, waits for them, and re-layouts  6.59 us (6%)
    pallas_call x1, Pallas kernels, rows_gather(): pl.pallas_call(kernel, out_shape=[jax.ShapeDtypeStruct((blocks,) + own.sh...  56.8 us
    pallas_call x1, Pallas kernels, block_scatter(): pl.pallas_call(kernel, out_shape=jax.ShapeDtypeStruct(block, kind), in_sp...  34.7 us

profile of v4, /device:TPU:6, one launch (start us, length us, event | category | flops | bytes accessed | tf_op | source)
XLA Modules:
  0.0 105.2 jit_solution(12381360122681169565)
XLA Ops:
  0.0 0.0 copy-start
  0.0 0.9 constant_dynamic-slice_fusion
  1.0 0.1 copy-done
  1.1 0.6 pad_maximum_fusion.2.catalog_own_ref
  1.7 0.8 fusion.3
  2.5 0.1 copy.14
  2.6 0.1 reduce-window.8
  2.7 0.1 add_reduce_fusion
  2.8 0.1 select_reduce_fusion.2
  2.9 1.0 broadcast_in_dim.81.choose_ref
  3.9 0.9 select_reduce_fusion
  4.8 0.1 select_reduce_fusion.1
  4.9 0.1 broadcast_in_dim.80
  5.0 1.0 fusion
  6.0 1.0 fusion.2
  7.0 0.6 pad_maximum_fusion.own_ref
  7.6 1.5 %pad_maximum_fusion.1.factor_ref = bf16[4,48,144]{2,1,0:T(8,128)(2,1)} fusion(bf16[4,16,144]{2,1,0:T(8,128)(2,1)} %bitcast.22, bf16[4,32,144]{2,1,0:T(8,128)(2,1)} %bitcast.20), kind=kLoop, calls=%fused_computation.8 | loop fusion | flops 110592 | bytes 110592 | tf_op jit(solution)/shard_map/concatenate | solution.py:538
  9.2 56.8 %rows_gather.1 = (bf16[32,32,1664]{2,1,0:T(8,128)(2,1)}, bf16[32,16,2304]{2,1,0:T(8,128)(2,1)}, bf16[16,4,48,144]{3,2,1,0:T(8,128)(2,1)}) custom-call(bf16[32,1664]{1,0:T(8,128)(2,1)} %pad_maximum_fusion.own_ref, bf16[4,2304]{1,0:T(4,128)(2,1)} %pad_maximum_fusion.2.catalog_own_ref, f32[64,16,128]{2,1,0:T(8,128)} %broadcast_in_dim.81.choose_ref, ...), custom_call_target="tpu_custom_call" | custom-call | tf_op jit(solution)/shard_map/rows_gather/pallas_call | solution.py:267
  66.0 2.0 %gather_fusion = bf16[16,48,144]{2,1,0:T(8,128)(2,1)S(1)} fusion(bf16[64,48,144]{2,1,0:T(8,128)(2,1)} %bitcast.19, s32[1024]{0:T(1024)S(1)} %pad_clamp_fusion), kind=kCustom, calls=%fused_computation | custom fusion | bytes 442432 | tf_op jit(solution)/shard_map/jit(_take)/gather | solution.py:546
  68.0 0.1 select_bitcast_fusion
  68.1 0.9 copy.15
  68.9 34.7 %block_scatter.1 = bf16[32,1536]{1,0:T(8,128)(2,1)} custom-call(bf16[32,32,1664]{2,1,0:T(8,128)(2,1)} %get-tuple-element.8.all_ref, bf16[32,16,2304]{2,1,0:T(8,128)(2,1)} %get-tuple-element.9.picks_ref, bf16[2,144,1536]{2,1,0:T(8,128)(2,1)} %gate_up_ref.1, bf16[3,256,144]{2,1,0:T(8,128)(2,1)} %bitcast.18, bf16[144,1536]{1,0:T(8,128)(2,1)} %down_ref.1, ...), custom_call_target="tpu_custom_call" | custom-call | tf_op jit(solution)/shard_map/block_scatter/pallas_call | solution.py:467
  103.7 1.5 %copy.23 = bf16[32,1536]{1,0:T(8,128)(2,1)} copy(bf16[32,1536]{1,0:T(8,128)(2,1)} %block_scatter.1) | data formatting | bytes 196608
  (10 shorter events, 0.1 us)
Async XLA Ops:
  0.0 1.0 copy-start

commit v5 on v4

--- a/solution.py
+++ b/solution.py
@@ -50,22 +50,46 @@
 ROWS, PICKS, FACTORS = 0, 1, 2
 
 
-def rows_gather(own, catalog_rows, choose, factors, holders):
+def sublayer(own, catalog_rows, choose, factors, active, gate_up, down, stream_rows, holders):
     blocks = 4 * RING
     kept, catalog_width = catalog_rows.shape
     chunk = catalog_width // 6
     picks = choose.shape[1]
+    rows, width = stream_rows.shape
+    factor_rows, hidden_dev = factors.shape[1:]
+    cat_rows = picks * factor_rows // 3
+    rank_pairs = blocks
+    kind = own.dtype
+    half = width // 2
+    minor = (((1,), (1,)), ((), ()))
 
     def kernel(
         own_ref,
         catalog_own_ref,
         choose_ref,
         factor_ref,
+        active_ref,
+        gate_up_ref,
+        down_ref,
+        stream_ref,
+        out_ref,
         all_ref,
         picks_all_ref,
         factor_all_ref,
         catalog_ref,
         picks_ref,
+        wide_low_ref,
+        wide_high_ref,
+        active_factor_ref,
+        group_ref,
+        rows_in_ref,
+        down_out_ref,
+        part_ref,
+        sib_ref,
+        leave_ref,
+        arrive_ref,
+        cross_out_ref,
+        cross_in_ref,
         ring_send,
         ring_recv,
         across_send,
@@ -75,6 +99,12 @@
         catalog_send,
         catalog_recv,
         local_sem,
+        sum_ring_send,
+        sum_ring_recv,
+        sum_across_send,
+        sum_across_recv,
+        sum_sib_send,
+        sum_sib_recv,
     ):
         me = lax.axis_index("blk")
         me_adp = lax.axis_index("adp")
@@ -198,7 +228,6 @@
             push(copy)
         keep = pltpu.make_async_copy(catalog_own_ref, catalog_ref.at[me_adp], local_sem.at[3])
         keep.start()
-        keeps.append(launch(FACTORS))
         relay(ROWS, OWN, 1)
         join(ROWS)
         relay(ROWS, OWN, 2)
@@ -209,6 +238,7 @@
                 slab, slab, catalog_send.at[step], catalog_recv.at[step], target
             ).wait_recv()
         keep.wait()
+        keeps.append(launch(FACTORS))
         for part in range(6):
             cols = slice(part * chunk, (part + 1) * chunk)
             total = jnp.zeros((picks, chunk), jnp.float32)
@@ -244,106 +274,37 @@
         relay(PICKS, OWN, 4)
         relay(FACTORS, OTHER, 4)
         relay(PICKS, OTHER, 4)
-        for kind in (ROWS, PICKS):
+        for keep in keeps:
+            keep.wait()
+        for place in range(picks):
+            number = active_ref[place]
+            slab = factor_all_ref[number // kept, lax.rem(number, kept)].astype(jnp.float32)
+            spare = jnp.zeros((factor_rows, 256 - hidden_dev), jnp.float32)
+            slab = jnp.concatenate([slab, spare], axis=1)
+            spots = pl.ds(place, factor_rows, stride=picks)
+            wide_low_ref[spots, :] = slab[:, :128]
+            wide_high_ref[spots, :] = slab[:, 128:]
+        wide = jnp.concatenate([wide_low_ref[...], wide_high_ref[...]], axis=1)[:, :hidden_dev]
+        active_factor_ref[...] = wide.astype(kind).reshape(active_factor_ref.shape)
+        for slabs in (ROWS, PICKS):
             for far in range(0, 5):
                 for stream in (OWN, OTHER):
                     for way in (FWD, BWD):
                         if far > reach(stream, way) or (far == 0 and way == BWD):
                             continue
-                        slab = landing[kind].at[index_of(kind, stream, way, far, 1 - core)]
+                        slab = landing[slabs].at[index_of(slabs, stream, way, far, 1 - core)]
                         remote(
                             slab,
                             slab,
-                            sib_send.at[kind, stream, way, far],
-                            sib_recv.at[kind, stream, way, far],
+                            sib_send.at[slabs, stream, way, far],
+                            sib_recv.at[slabs, stream, way, far],
                             sibling,
                         ).wait_recv()
-        for copy in sent:
-            copy.wait_send()
-        for keep in keeps:
-            keep.wait()
-
-    dma = pltpu.SemaphoreType.DMA
-    return pl.pallas_call(
-        kernel,
-        out_shape=[
-            jax.ShapeDtypeStruct((blocks,) + own.shape, own.dtype),
-            jax.ShapeDtypeStruct((blocks, picks, catalog_width), own.dtype),
-            jax.ShapeDtypeStruct((holders,) + factors.shape, factors.dtype),
-        ],
-        in_specs=[pl.BlockSpec(memory_space=pltpu.VMEM)] * 4,
-        out_specs=[pl.BlockSpec(memory_space=pltpu.VMEM)] * 3,
-        scratch_shapes=[
-            pltpu.VMEM((holders, kept, catalog_width), own.dtype),
-            pltpu.VMEM((picks, catalog_width), own.dtype),
-            dma((3, 2, 2, 4)),
-            dma((3, 2, 2, 4)),
-            dma((3,)),
-            dma((3,)),
-            dma((2, 2, 2, 5)),
-            dma((2, 2, 2, 5)),
-            dma((holders - 1,)),
-            dma((holders - 1,)),
-            dma((4,)),
-        ],
-        compiler_params=pltpu.CompilerParams(collective_id=2, has_side_effects=True),
-        name="rows_gather",
-    )(own, catalog_rows, choose, factors)
-
-
-def block_scatter(gathered, picks, gate_up, factors, down, stream_rows):
-    rows, width = stream_rows.shape
-    rank_pairs = gathered.shape[0]
-    cat_rows = factors.shape[1]
-    kind = gathered.dtype
-    half = width // 2
-    minor = (((1,), (1,)), ((), ()))
-
-    def kernel(
-        all_ref,
-        picks_ref,
-        gate_up_ref,
-        factor_ref,
-        down_ref,
-        stream_ref,
-        out_ref,
-        group_ref,
-        rows_in_ref,
-        down_out_ref,
-        part_ref,
-        sib_ref,
-        leave_ref,
-        arrive_ref,
-        cross_out_ref,
-        cross_in_ref,
-        ring_send,
-        ring_recv,
-        across_send,
-        across_recv,
-        sib_send,
-        sib_recv,
-    ):
-        me = lax.axis_index("blk")
-        x_hi = me // (2 * RING)
-        z = lax.rem(me // 2, RING)
-        core = lax.rem(me, 2)
-        sibling = {"blk": blk_index(x_hi, z, 1 - core)}
-        across = {"blk": blk_index(1 - x_hi, z, core)}
-        ahead = {
-            FWD: {"blk": blk_index(x_hi, lax.rem(z + 1, RING), core)},
-            BWD: {"blk": blk_index(x_hi, lax.rem(z + RING - 1, RING), core)},
-        }
-        greet([sibling, across, ahead[FWD], ahead[BWD]])
-        sent = []
 
         def at(stream, way, far, owner_core):
             x_of = x_hi if stream == OWN else 1 - x_hi
             z_of = lax.rem(z + far, RING) if way == FWD else lax.rem(z + RING - far, RING)
             return blk_index(x_of, z_of, owner_core)
-
-        def push(copy):
-            copy.start()
-            sent.append(copy)
 
         def keys_at(far):
             return [
@@ -357,15 +318,15 @@
             return remote(
                 part_ref.at[1, stream, way, far],
                 sib_ref.at[stream, way, far],
-                sib_send.at[stream, way, far],
-                sib_recv.at[stream, way, far],
+                sum_sib_send.at[stream, way, far],
+                sum_sib_recv.at[stream, way, far],
                 sibling,
             )
 
         for k in range(rank_pairs):
-            rows_in_ref[k * ACTIVE : (k + 1) * ACTIVE, :] = picks_ref[k, :, :width]
+            rows_in_ref[k * ACTIVE : (k + 1) * ACTIVE, :] = picks_all_ref[k, :, :width]
             rank, start = k // 2, (k % 2) * half
-            down_out_ref[rank * ACTIVE : (rank + 1) * ACTIVE, start : start + half] = picks_ref[
+            down_out_ref[rank * ACTIVE : (rank + 1) * ACTIVE, start : start + half] = picks_all_ref[
                 k, :, width:
             ]
 
@@ -400,11 +361,11 @@
                 )
                 pre.append(
                     base
-                    + jnp.dot(spread(low), factor_ref[side], preferred_element_type=jnp.float32)
+                    + jnp.dot(spread(low), active_factor_ref[side], preferred_element_type=jnp.float32)
                 )
             hidden = (jax.nn.gelu(pre[0], approximate=True) * pre[1]).astype(kind)
             low = lax.dot_general(
-                hidden, factor_ref[2], minor, preferred_element_type=jnp.float32
+                hidden, active_factor_ref[2], minor, preferred_element_type=jnp.float32
             )
             part = jnp.dot(hidden, down_ref[...], preferred_element_type=jnp.float32) + jnp.dot(
                 spread(low), down_out_ref[...], preferred_element_type=jnp.float32
@@ -424,9 +385,9 @@
             return remote(
                 leave_ref.at[stream, way, far - 1],
                 arrive_ref.at[stream, way, far - 1],
-                ring_send.at[stream, way, far - 1],
-                ring_recv.at[stream, way, far - 1],
-                ahead[way],
+                sum_ring_send.at[stream, way, far - 1],
+                sum_ring_recv.at[stream, way, far - 1],
+                blk_ahead[way],
             )
 
         def arrived(stream, way, far):
@@ -442,7 +403,7 @@
                     total = total + arrived(stream, FWD, 0) + arrived(stream, BWD, 0)
                     if stream == OTHER:
                         cross_out_ref[...] = total.astype(kind)
-                        push(remote(cross_out_ref, cross_in_ref, across_send, across_recv, across))
+                        push(remote(cross_out_ref, cross_in_ref, sum_across_send, sum_across_recv, blk_across))
                     else:
                         totals[stream] = total
                     continue
@@ -456,7 +417,7 @@
             compute(far)
             pass_on(far + 1)
         pass_on(0)
-        remote(cross_out_ref, cross_in_ref, across_send, across_recv, across).wait_recv()
+        remote(cross_out_ref, cross_in_ref, sum_across_send, sum_across_recv, blk_across).wait_recv()
         total = totals[OWN] + cross_in_ref[...].astype(jnp.float32)
         out_ref[...] = (stream_ref[...].astype(jnp.float32) + total).astype(kind)
         for copy in sent:
@@ -464,12 +425,21 @@
 
     dma = pltpu.SemaphoreType.DMA
     block = (rows, width)
+    vmem = pl.BlockSpec(memory_space=pltpu.VMEM)
     return pl.pallas_call(
         kernel,
         out_shape=jax.ShapeDtypeStruct(block, kind),
-        in_specs=[pl.BlockSpec(memory_space=pltpu.VMEM)] * 6,
-        out_specs=pl.BlockSpec(memory_space=pltpu.VMEM),
+        in_specs=[vmem] * 4 + [pl.BlockSpec(memory_space=pltpu.SMEM)] + [vmem] * 3,
+        out_specs=vmem,
         scratch_shapes=[
+            pltpu.VMEM((blocks,) + own.shape, kind),
+            pltpu.VMEM((blocks, picks, catalog_width), kind),
+            pltpu.VMEM((holders,) + factors.shape, kind),
+            pltpu.VMEM((holders, kept, catalog_width), kind),
+            pltpu.VMEM((picks, catalog_width), kind),
+            pltpu.VMEM((picks * factor_rows, 128), jnp.float32),
+            pltpu.VMEM((picks * factor_rows, 128), jnp.float32),
+            pltpu.VMEM((3, cat_rows, hidden_dev), kind),
             pltpu.VMEM((8 * rows, width), kind),
             pltpu.VMEM((2 * cat_rows, width), kind),
             pltpu.VMEM((cat_rows, width), kind),
@@ -479,6 +449,15 @@
             pltpu.VMEM((2, 2, 4) + block, kind),
             pltpu.VMEM(block, kind),
             pltpu.VMEM(block, kind),
+            dma((3, 2, 2, 4)),
+            dma((3, 2, 2, 4)),
+            dma((3,)),
+            dma((3,)),
+            dma((2, 2, 2, 5)),
+            dma((2, 2, 2, 5)),
+            dma((holders - 1,)),
+            dma((holders - 1,)),
+            dma((4,)),
             dma((2, 2, 4)),
             dma((2, 2, 4)),
             dma,
@@ -486,9 +465,9 @@
             dma((2, 2, 5)),
             dma((2, 2, 5)),
         ],
-        compiler_params=pltpu.CompilerParams(collective_id=3, has_side_effects=True),
-        name="block_scatter",
-    )(gathered, picks, gate_up, factors, down, stream_rows)
+        compiler_params=pltpu.CompilerParams(collective_id=1, has_side_effects=True),
+        name="sublayer",
+    )(own, catalog_rows, choose, factors, active, gate_up, down, stream_rows)
 
 
 def local(
@@ -542,13 +521,17 @@
         ],
         axis=1,
     )
-    gathered, picks, factors = rows_gather(packed, catalog_rows, choose, own_factors, holders)
-    factors = jnp.take(
-        factors.reshape(kept_rows * holders, 3 * rank_columns, hidden_dev), active, axis=0
-    ).transpose(1, 0, 2)
-    cat_rows = ACTIVE * rank_columns
-    factors = factors.reshape(3, cat_rows, hidden_dev)
-    return block_scatter(gathered, picks, gate_up_weight, factors, down_weight, stream)
+    return sublayer(
+        packed,
+        catalog_rows,
+        choose,
+        own_factors,
+        active,
+        gate_up_weight,
+        down_weight,
+        stream,
+        holders,
+    )
 
 
 def solution(mesh):

time: 106 us -> 95 us (0.90)
  the two profiles are of different devices: /device:TPU:6 before, /device:TPU:64 now
where the time goes in v5:
time: 95 us; the launch traced here: 94.6 us
  Pallas kernels  84.6 us (89%)
  local copies, waits for them, and re-layouts  6.2 us (7%)
  other arithmetic  3.75 us (4%)
    pallas_call x1, Pallas kernels, sublayer(): pl.pallas_call(kernel, out_shape=jax.ShapeDtypeStruct(block, kind), in_sp...  84.6 us
    unnamed x19, local copies, waits for them, and re-layouts  4.1 us

profile of v5, /device:TPU:64, one launch (start us, length us, event | category | flops | bytes accessed | tf_op | source)
XLA Modules:
  0.0 94.6 jit_solution(15581298392915850)
XLA Ops:
  0.0 0.0 copy-start
  0.0 0.0 copy-start.6
  0.0 0.7 copy-done.6
  0.7 0.1 fusion.3
  0.8 0.0 copy-start.7
  0.9 0.6 copy-done.7
  1.5 0.2 select_reduce_fusion
  1.7 1.0 %fusion = f32[32]{0:T(128)S(1)} fusion(bf16[32,1536]{1,0:T(8,128)(2,1)} %stream_ref.1), kind=kLoop, calls=%fused_computation.2 | loop fusion | flops 147424 | bytes 98432 | tf_op jit(solution)/shard_map/reduce_sum | solution.py:18
  2.7 0.9 constant_dynamic-slice_fusion.1
  3.6 0.0 copy-done
  3.7 0.6 pad_maximum_fusion.2.catalog_own_ref
  4.3 0.0 copy-start.1
  4.3 0.1 copy.13
  4.4 0.1 reduce-window.8
  4.5 0.1 add_reduce_fusion
  4.6 0.1 select_reduce_fusion.2.active_ref
  4.7 0.0 copy-start.5
  4.7 0.1 select_reduce_fusion.1
  4.8 0.1 broadcast_in_dim.46
  4.9 0.3 copy-done.5
  5.2 0.0 copy-start.4
  5.2 0.0 copy-done.1
  5.3 0.7 copy-done.4
  5.9 0.1 fusion.2
  6.0 0.0 copy-start.2
  6.0 0.0 copy-start.3
  6.0 0.6 pad_maximum_fusion.own_ref
  6.7 0.2 copy-done.2
  6.9 0.0 copy-done.3
  6.9 0.7 pad_maximum_fusion.1.factor_ref
  7.5 1.0 %broadcast_in_dim.47.choose_ref = f32[64,16,128]{2,1,0:T(8,128)} broadcast(f32[64,16]{1,0:T(8,128)S(1)} %fusion.4), dimensions={0,1} | broadcast | bytes 528384 | tf_op jit(solution)/shard_map/broadcast_in_dim | solution.py:513
  8.5 84.6 %sublayer.1 = bf16[32,1536]{1,0:T(8,128)(2,1)} custom-call(bf16[32,1664]{1,0:T(8,128)(2,1)} %pad_maximum_fusion.own_ref, bf16[4,2304]{1,0:T(4,128)(2,1)} %pad_maximum_fusion.2.catalog_own_ref, f32[64,16,128]{2,1,0:T(8,128)} %broadcast_in_dim.47.choose_ref, bf16[4,48,144]{2,1,0:T(8,128)(2,1)} %pad_maximum_fusion.1.factor_ref, s32[16]{0:T(128)} %copy-done.5, ...), custom_call_target="tpu_custom_call" | custom-call | tf_op jit(solution)/shard_map/sublayer/pallas_call | solution.py:429
  93.1 1.5 %copy.21 = bf16[32,1536]{1,0:T(8,128)(2,1)} copy(bf16[32,1536]{1,0:T(8,128)(2,1)} %sublayer.1) | data formatting | bytes 196608
  (7 shorter events, 0.1 us)
Async XLA Ops:
  0.0 3.6 %copy-start = (bf16[4,32,1536]{2,1,0:T(8,128)(2,1)S(1)}, bf16[4,32,1536]{2,1,0:T(8,128)(2,1)}, u32[]{:S(2)}) copy-start(bf16[4,32,1536]{2,1,0:T(8,128)(2,1)} %param.14) | copy-start | bytes 1179652
  0.0 0.7 copy-start.6
  0.8 0.7 copy-start.7
  4.3 0.9 copy-start.1
  4.7 0.5 copy-start.5
  5.2 0.7 copy-start.4
  6.0 0.8 copy-start.2
  6.0 0.8 copy-start.3

commit v6 on v5

--- a/solution.py
+++ b/solution.py
@@ -29,7 +29,6 @@
         pl.semaphore_signal(
             barrier, inc=1, device_id=target, device_id_type=pl.DeviceIdType.MESH
         )
-    pl.semaphore_wait(barrier, len(targets))
 
 
 def remote(src, dst, send_sem, recv_sem, target):
@@ -50,29 +49,47 @@
 ROWS, PICKS, FACTORS = 0, 1, 2
 
 
-def sublayer(own, catalog_rows, choose, factors, active, gate_up, down, stream_rows, holders):
+def sublayer(
+    stream_rows,
+    gain,
+    slots,
+    gate_in,
+    down_out,
+    active_rows,
+    factors,
+    active,
+    gate_up,
+    down,
+    holders,
+):
     blocks = 4 * RING
-    kept, catalog_width = catalog_rows.shape
+    kept = gate_in.shape[0]
+    rows, width = stream_rows.shape
+    packed_width = width + slots.shape[1]
+    catalog_width = width + width // 2
     chunk = catalog_width // 6
-    picks = choose.shape[1]
-    rows, width = stream_rows.shape
+    picks = active_rows.shape[0]
     factor_rows, hidden_dev = factors.shape[1:]
     cat_rows = picks * factor_rows // 3
     rank_pairs = blocks
-    kind = own.dtype
+    kind = stream_rows.dtype
     half = width // 2
     minor = (((1,), (1,)), ((), ()))
 
     def kernel(
-        own_ref,
-        catalog_own_ref,
-        choose_ref,
+        stream_ref,
+        gain_ref,
+        slots_ref,
+        gate_in_ref,
+        down_out_ref,
+        active_rows_ref,
         factor_ref,
         active_ref,
         gate_up_ref,
         down_ref,
-        stream_ref,
         out_ref,
+        own_ref,
+        catalog_own_ref,
         all_ref,
         picks_all_ref,
         factor_all_ref,
@@ -82,8 +99,6 @@
         wide_high_ref,
         active_factor_ref,
         group_ref,
-        rows_in_ref,
-        down_out_ref,
         part_ref,
         sib_ref,
         leave_ref,
@@ -129,7 +144,25 @@
         ahead = [blk_ahead, blk_ahead, adp_ahead]
         source = [own_ref, picks_ref, factor_ref]
         landing = [all_ref, picks_all_ref, factor_all_ref]
-        greet([sibling, blk_across, blk_ahead[FWD], blk_ahead[BWD]] + adp_peers)
+        greeted = [sibling, blk_across, blk_ahead[FWD], blk_ahead[BWD]] + adp_peers
+        greet(greeted)
+
+        def pick_row(table, at_row):
+            place = lax.broadcasted_iota(jnp.int32, table.shape, 0)
+            kept_row = jnp.where(place == at_row, table.astype(jnp.float32), 0.0)
+            return jnp.sum(kept_row, axis=0, keepdims=True)
+
+        out_rows = [pick_row(down_out_ref[row], me // 2) for row in range(kept)]
+        in_rows = [pick_row(gate_in_ref[row], me) for row in range(kept)]
+        in_rows = jnp.concatenate(in_rows, axis=0)
+        out_rows = jnp.concatenate(out_rows, axis=0)
+        catalog_own_ref[:, :width] = in_rows.astype(kind)
+        catalog_own_ref[:, width:] = jnp.where(
+            core == 0, out_rows[:, :half], out_rows[:, half:]
+        ).astype(kind)
+        own_ref[:, :width] = normalize(stream_ref[...], gain_ref[...])
+        own_ref[:, width:] = slots_ref[...]
+        pl.semaphore_wait(pltpu.get_barrier_semaphore(), len(greeted))
         sent = []
 
         def around(at, way, far):
@@ -216,7 +249,7 @@
                     to_ring(slab, index, kind, stream, way, far)
                 to_sibling(slab, index, kind, stream, way, far)
 
-        keeps = [launch(ROWS)]
+        keeps = []
         for step, target in enumerate(adp_peers):
             copy = remote(
                 catalog_own_ref,
@@ -226,6 +259,7 @@
                 target,
             )
             push(copy)
+        keeps.append(launch(ROWS))
         keep = pltpu.make_async_copy(catalog_own_ref, catalog_ref.at[me_adp], local_sem.at[3])
         keep.start()
         relay(ROWS, OWN, 1)
@@ -245,7 +279,9 @@
             for holder in range(holders):
                 held = catalog_ref[holder, :, cols].astype(jnp.float32)
                 for row in range(kept):
-                    mask = jnp.concatenate([choose_ref[holder * kept + row]] * (chunk // 128), axis=1)
+                    number = float(holder * kept + row)
+                    mask = jnp.where(active_rows_ref[...] == number, 1.0, 0.0)
+                    mask = jnp.concatenate([mask] * (chunk // 128), axis=1)
                     total = total + mask * held[row : row + 1, :]
             picks_ref[:, cols] = total.astype(picks_ref.dtype)
 
@@ -273,20 +309,12 @@
         relay(PICKS, OTHER, 3)
         relay(PICKS, OWN, 4)
         relay(FACTORS, OTHER, 4)
-        relay(PICKS, OTHER, 4)
-        for keep in keeps:
-            keep.wait()
-        for place in range(picks):
-            number = active_ref[place]
-            slab = factor_all_ref[number // kept, lax.rem(number, kept)].astype(jnp.float32)
-            spare = jnp.zeros((factor_rows, 256 - hidden_dev), jnp.float32)
-            slab = jnp.concatenate([slab, spare], axis=1)
-            spots = pl.ds(place, factor_rows, stride=picks)
-            wide_low_ref[spots, :] = slab[:, :128]
-            wide_high_ref[spots, :] = slab[:, 128:]
-        wide = jnp.concatenate([wide_low_ref[...], wide_high_ref[...]], axis=1)[:, :hidden_dev]
-        active_factor_ref[...] = wide.astype(kind).reshape(active_factor_ref.shape)
-        for slabs in (ROWS, PICKS):
+        def at(stream, way, far, owner_core):
+            x_of = x_hi if stream == OWN else 1 - x_hi
+            z_of = lax.rem(z + far, RING) if way == FWD else lax.rem(z + RING - far, RING)
+            return blk_index(x_of, z_of, owner_core)
+
+        def settle(slabs):
             for far in range(0, 5):
                 for stream in (OWN, OTHER):
                     for way in (FWD, BWD):
@@ -301,11 +329,6 @@
                             sibling,
                         ).wait_recv()
 
-        def at(stream, way, far, owner_core):
-            x_of = x_hi if stream == OWN else 1 - x_hi
-            z_of = lax.rem(z + far, RING) if way == FWD else lax.rem(z + RING - far, RING)
-            return blk_index(x_of, z_of, owner_core)
-
         def keys_at(far):
             return [
                 (stream, way, far)
@@ -323,21 +346,29 @@
                 sibling,
             )
 
-        for k in range(rank_pairs):
-            rows_in_ref[k * ACTIVE : (k + 1) * ACTIVE, :] = picks_all_ref[k, :, :width]
-            rank, start = k // 2, (k % 2) * half
-            down_out_ref[rank * ACTIVE : (rank + 1) * ACTIVE, start : start + half] = picks_all_ref[
-                k, :, width:
+        def slots_at(far):
+            return [(side,) + key for side in (1, 0) for key in keys_at(far)]
+
+        def base_of(far):
+            slots = slots_at(far)
+            for place, (side, stream, way, _) in enumerate(slots):
+                index = at(stream, way, far, core if side == 0 else 1 - core)
+                group_ref[place * rows : (place + 1) * rows, :] = all_ref[index, :, :width]
+            group = group_ref[: len(slots) * rows, :]
+            return [
+                lax.dot_general(
+                    group, gate_up_ref[side], minor, preferred_element_type=jnp.float32
+                )
+                for side in range(2)
             ]
 
-        def compute(far):
+        def compute(far, base):
             keys = keys_at(far)
-            slots = [(side,) + key for side in (1, 0) for key in keys]
+            slots = slots_at(far)
             count = len(slots) * rows
             numbers = []
             for place, (side, stream, way, _) in enumerate(slots):
                 index = at(stream, way, far, core if side == 0 else 1 - core)
-                group_ref[place * rows : (place + 1) * rows, :] = all_ref[index, :, :width]
                 numbers.append(all_ref[index, :, width:].astype(jnp.float32))
             number = jnp.concatenate(numbers, axis=0)
             number = jnp.concatenate([number] * (cat_rows // number.shape[1]), axis=1)
@@ -352,23 +383,38 @@
             for side in range(2):
                 low = lax.dot_general(
                     group,
-                    rows_in_ref[side * cat_rows : (side + 1) * cat_rows, :],
+                    picks_all_ref[side * picks : (side + 1) * picks, :, :width].reshape(
+                        cat_rows, width
+                    ),
                     minor,
                     preferred_element_type=jnp.float32,
                 )
-                base = lax.dot_general(
-                    group, gate_up_ref[side], minor, preferred_element_type=jnp.float32
-                )
                 pre.append(
-                    base
+                    base[side]
                     + jnp.dot(spread(low), active_factor_ref[side], preferred_element_type=jnp.float32)
                 )
             hidden = (jax.nn.gelu(pre[0], approximate=True) * pre[1]).astype(kind)
             low = lax.dot_general(
                 hidden, active_factor_ref[2], minor, preferred_element_type=jnp.float32
             )
-            part = jnp.dot(hidden, down_ref[...], preferred_element_type=jnp.float32) + jnp.dot(
-                spread(low), down_out_ref[...], preferred_element_type=jnp.float32
+            low_spread = spread(low)
+            part = jnp.dot(hidden, down_ref[...], preferred_element_type=jnp.float32)
+            part = part + jnp.concatenate(
+                [
+                    jnp.dot(
+                        low_spread,
+                        jnp.concatenate(
+                            [
+                                picks_all_ref[k, :, width:]
+                                for k in range(side, rank_pairs, 2)
+                            ],
+                            axis=0,
+                        ),
+                        preferred_element_type=jnp.float32,
+                    )
+                    for side in range(2)
+                ],
+                axis=1,
             )
             part = part.astype(kind)
             for place, slot in enumerate(slots):
@@ -412,9 +458,25 @@
                 leave_ref[stream, way, far - 1] = total.astype(kind)
                 push(ring_copy(stream, way, far))
 
-        compute(4)
+        for keep in keeps:
+            keep.wait()
+        for place in range(picks):
+            number = active_ref[place]
+            slab = factor_all_ref[number // kept, lax.rem(number, kept)].astype(jnp.float32)
+            spare = jnp.zeros((factor_rows, 256 - hidden_dev), jnp.float32)
+            slab = jnp.concatenate([slab, spare], axis=1)
+            spots = pl.ds(place, factor_rows, stride=picks)
+            wide_low_ref[spots, :] = slab[:, :128]
+            wide_high_ref[spots, :] = slab[:, 128:]
+        wide = jnp.concatenate([wide_low_ref[...], wide_high_ref[...]], axis=1)[:, :hidden_dev]
+        active_factor_ref[...] = wide.astype(kind).reshape(active_factor_ref.shape)
+        settle(ROWS)
+        first_base = base_of(4)
+        relay(PICKS, OTHER, 4)
+        settle(PICKS)
+        compute(4, first_base)
         for far in range(3, -1, -1):
-            compute(far)
+            compute(far, base_of(far))
             pass_on(far + 1)
         pass_on(0)
         remote(cross_out_ref, cross_in_ref, sum_across_send, sum_across_recv, blk_across).wait_recv()
@@ -429,10 +491,12 @@
     return pl.pallas_call(
         kernel,
         out_shape=jax.ShapeDtypeStruct(block, kind),
-        in_specs=[vmem] * 4 + [pl.BlockSpec(memory_space=pltpu.SMEM)] + [vmem] * 3,
+        in_specs=[vmem] * 7 + [pl.BlockSpec(memory_space=pltpu.SMEM)] + [vmem] * 2,
         out_specs=vmem,
         scratch_shapes=[
-            pltpu.VMEM((blocks,) + own.shape, kind),
+            pltpu.VMEM((rows, packed_width), kind),
+            pltpu.VMEM((kept, catalog_width), kind),
+            pltpu.VMEM((blocks, rows, packed_width), kind),
             pltpu.VMEM((blocks, picks, catalog_width), kind),
             pltpu.VMEM((holders,) + factors.shape, kind),
             pltpu.VMEM((holders, kept, catalog_width), kind),
@@ -441,8 +505,6 @@
             pltpu.VMEM((picks * factor_rows, 128), jnp.float32),
             pltpu.VMEM((3, cat_rows, hidden_dev), kind),
             pltpu.VMEM((8 * rows, width), kind),
-            pltpu.VMEM((2 * cat_rows, width), kind),
-            pltpu.VMEM((cat_rows, width), kind),
             pltpu.VMEM((2, 2, 2, 5) + block, kind),
             pltpu.VMEM((2, 2, 5) + block, kind),
             pltpu.VMEM((2, 2, 4) + block, kind),
@@ -467,7 +529,18 @@
         ],
         compiler_params=pltpu.CompilerParams(collective_id=1, has_side_effects=True),
         name="sublayer",
-    )(own, catalog_rows, choose, factors, active, gate_up, down, stream_rows)
+    )(
+        stream_rows,
+        gain,
+        slots,
+        gate_in,
+        down_out,
+        active_rows,
+        factors,
+        active,
+        gate_up,
+        down,
+    )
 
 
 def local(
@@ -501,19 +574,6 @@
     )
     own_match = own_adapter[:, None] == active[None, :]
     own_slot = jnp.sum(jnp.where(own_match, active_pos[None, :], 0), axis=1)
-    normed = normalize(stream, prenorm_gain)
-    place = lax.axis_index("blk")
-    half = width // 2
-    row_in = lax.dynamic_slice_in_dim(adapter_gate_input, place, 1, axis=1)[:, 0]
-    row_out = lax.dynamic_slice(
-        adapter_down_output, (0, place // 2, lax.rem(place, 2) * half), (kept_rows, 1, half)
-    )[:, 0]
-    catalog_rows = jnp.concatenate([row_in, row_out], axis=1)
-    choose = (catalog[:, None] == active[None, :]).astype(jnp.float32)
-    choose = jnp.broadcast_to(choose[:, :, None], choose.shape + (128,))
-    packed = jnp.concatenate(
-        [normed, jnp.broadcast_to(own_slot.astype(jnp.bfloat16)[:, None], (tok_rows, 128))], axis=1
-    )
     own_factors = jnp.concatenate(
         [
             adapter_gate_output.reshape(kept_rows, 2 * rank_columns, hidden_dev),
@@ -521,15 +581,19 @@
         ],
         axis=1,
     )
+    slots = jnp.broadcast_to(own_slot.astype(jnp.bfloat16)[:, None], (tok_rows, 128))
+    active_rows = jnp.broadcast_to(active.astype(jnp.float32)[:, None], (ACTIVE, 128))
     return sublayer(
-        packed,
-        catalog_rows,
-        choose,
+        stream,
+        prenorm_gain[None, :],
+        slots,
+        adapter_gate_input,
+        adapter_down_output,
+        active_rows,
         own_factors,
         active,
         gate_up_weight,
         down_weight,
-        stream,
         holders,
     )
 

time: 95 us -> 90.2 us (0.949)
  the two profiles are of different devices: /device:TPU:64 before, /device:TPU:6 now
where the time goes in v6:
time: 90.2 us; the launch traced here: 90 us
  Pallas kernels  83.1 us (92%)
  local copies, waits for them, and re-layouts  4.07 us (5%)
  other arithmetic  2.74 us (3%)
    pallas_call x1, Pallas kernels, sublayer(): pl.pallas_call(kernel, out_shape=jax.ShapeDtypeStruct(block, kind), in_sp...  83.1 us
    unnamed x9, local copies, waits for them, and re-layouts  2.03 us

profile of v6, /device:TPU:6, one launch (start us, length us, event | category | flops | bytes accessed | tf_op | source)
XLA Modules:
  0.0 90.0 jit_solution(9257092469818197888)
XLA Ops:
  0.0 0.0 copy-start.2
  0.0 0.8 fusion
  0.8 0.9 select_reduce_fusion
  1.7 0.0 copy-done.2
  1.7 0.6 broadcast_in_dim.42.gain_ref
  2.3 0.1 copy.13
  2.4 0.0 copy-start
  2.4 0.1 reduce-window.8
  2.5 0.0 copy-start.1
  2.5 0.1 add_reduce_fusion
  2.6 0.1 select_reduce_fusion.2.active_ref
  2.7 0.0 copy-start.3
  2.7 0.1 select_reduce_fusion.1
  2.8 0.5 copy-done.3
  3.3 0.7 broadcast_in_dim.71.active_rows_ref
  4.0 0.7 broadcast_in_dim.70.slots_ref
  4.7 0.0 copy-done
  4.7 0.0 copy-done.1
  4.7 0.7 pad_maximum_fusion.factor_ref
  5.3 83.1 %sublayer.1 = bf16[32,1536]{1,0:T(8,128)(2,1)} custom-call(bf16[32,1536]{1,0:T(8,128)(2,1)} %stream_ref.1, f32[1,1536]{1,0:T(1,128)} %broadcast_in_dim.42.gain_ref, bf16[32,128]{1,0:T(8,128)(2,1)} %broadcast_in_dim.70.slots_ref, bf16[4,32,1536]{2,1,0:T(8,128)(2,1)} %gate_in_ref.1, bf16[4,16,1536]{2,1,0:T(8,128)(2,1)} %down_out_ref.1, ...), custom_call_target="tpu_custom_call" | custom-call | tf_op jit(solution)/shard_map/sublayer/pallas_call | solution.py:491
  88.5 1.5 %copy.15 = bf16[32,1536]{1,0:T(8,128)(2,1)} copy(bf16[32,1536]{1,0:T(8,128)(2,1)} %sublayer.1) | data formatting | bytes 196608
  (3 shorter events, 0.0 us)
Async XLA Ops:
  0.0 1.7 %copy-start.2 = (f32[1536]{0:T(1024)S(1)}, f32[1536]{0:T(1024)}, u32[]{:S(2)}) copy-start(f32[1536]{0:T(1024)} %param.11) | copy-start | bytes 18436
  2.4 2.3 %copy-start = (bf16[4,2,16,144]{3,2,1,0:T(8,128)(2,1)S(1)}, bf16[4,2,16,144]{3,2,1,0:T(8,128)(2,1)}, u32[]{:S(2)}) copy-start(bf16[4,2,16,144]{3,2,1,0:T(8,128)(2,1)} %param.15) | copy-start | bytes 110596
  2.5 2.2 %copy-start.1 = (bf16[4,144,16]{1,2,0:T(8,128)(2,1)S(1)}, bf16[4,144,16]{1,2,0:T(8,128)(2,1)}, u32[]{:S(2)}) copy-start(bf16[4,144,16]{1,2,0:T(8,128)(2,1)} %param.16) | copy-start | bytes 55300
  2.7 0.6 copy-start.3

commit v7 on v6

--- a/solution.py
+++ b/solution.py
@@ -52,10 +52,9 @@
 def sublayer(
     stream_rows,
     gain,
-    slots,
+    numbers,
     gate_in,
     down_out,
-    active_rows,
     factors,
     active,
     gate_up,
@@ -65,10 +64,10 @@
     blocks = 4 * RING
     kept = gate_in.shape[0]
     rows, width = stream_rows.shape
-    packed_width = width + slots.shape[1]
+    packed_width = width + numbers.shape[1]
     catalog_width = width + width // 2
     chunk = catalog_width // 6
-    picks = active_rows.shape[0]
+    picks = numbers.shape[0] - rows
     factor_rows, hidden_dev = factors.shape[1:]
     cat_rows = picks * factor_rows // 3
     rank_pairs = blocks
@@ -79,10 +78,9 @@
     def kernel(
         stream_ref,
         gain_ref,
-        slots_ref,
+        numbers_ref,
         gate_in_ref,
         down_out_ref,
-        active_rows_ref,
         factor_ref,
         active_ref,
         gate_up_ref,
@@ -161,7 +159,7 @@
             core == 0, out_rows[:, :half], out_rows[:, half:]
         ).astype(kind)
         own_ref[:, :width] = normalize(stream_ref[...], gain_ref[...])
-        own_ref[:, width:] = slots_ref[...]
+        own_ref[:, width:] = numbers_ref[:rows, :].astype(kind)
         pl.semaphore_wait(pltpu.get_barrier_semaphore(), len(greeted))
         sent = []
 
@@ -280,7 +278,7 @@
                 held = catalog_ref[holder, :, cols].astype(jnp.float32)
                 for row in range(kept):
                     number = float(holder * kept + row)
-                    mask = jnp.where(active_rows_ref[...] == number, 1.0, 0.0)
+                    mask = jnp.where(numbers_ref[rows:, :] == number, 1.0, 0.0)
                     mask = jnp.concatenate([mask] * (chunk // 128), axis=1)
                     total = total + mask * held[row : row + 1, :]
             picks_ref[:, cols] = total.astype(picks_ref.dtype)
@@ -476,8 +474,9 @@
         settle(PICKS)
         compute(4, first_base)
         for far in range(3, -1, -1):
-            compute(far, base_of(far))
+            base = base_of(far)
             pass_on(far + 1)
+            compute(far, base)
         pass_on(0)
         remote(cross_out_ref, cross_in_ref, sum_across_send, sum_across_recv, blk_across).wait_recv()
         total = totals[OWN] + cross_in_ref[...].astype(jnp.float32)
@@ -491,7 +490,7 @@
     return pl.pallas_call(
         kernel,
         out_shape=jax.ShapeDtypeStruct(block, kind),
-        in_specs=[vmem] * 7 + [pl.BlockSpec(memory_space=pltpu.SMEM)] + [vmem] * 2,
+        in_specs=[vmem] * 6 + [pl.BlockSpec(memory_space=pltpu.SMEM)] + [vmem] * 2,
         out_specs=vmem,
         scratch_shapes=[
             pltpu.VMEM((rows, packed_width), kind),
@@ -532,10 +531,9 @@
     )(
         stream_rows,
         gain,
-        slots,
+        numbers,
         gate_in,
         down_out,
-        active_rows,
         factors,
         active,
         gate_up,
@@ -581,15 +579,14 @@
         ],
         axis=1,
     )
-    slots = jnp.broadcast_to(own_slot.astype(jnp.bfloat16)[:, None], (tok_rows, 128))
-    active_rows = jnp.broadcast_to(active.astype(jnp.float32)[:, None], (ACTIVE, 128))
+    numbers = jnp.concatenate([own_slot, active]).astype(jnp.float32)
+    numbers = jnp.broadcast_to(numbers[:, None], (tok_rows + ACTIVE, 128))
     return sublayer(
         stream,
-        prenorm_gain[None, :],
-        slots,
+        prenorm_gain,
+        numbers,
         adapter_gate_input,
         adapter_down_output,
-        active_rows,
         own_factors,
         active,
         gate_up_weight,

time: 90.2 us -> 90.8 us (level)
  the two profiles are of different devices: /device:TPU:6 before, /device:TPU:1 now
where the time goes in v7:
time: 90.8 us; the launch traced here: 90.6 us
  Pallas kernels  85.1 us (94%)
  local copies, waits for them, and re-layouts  4.06 us (4%)
  other arithmetic  1.43 us (2%)
    pallas_call x1, Pallas kernels, sublayer(): pl.pallas_call(kernel, out_shape=jax.ShapeDtypeStruct(block, kind), in_sp...  85.1 us
    unnamed x11, local copies, waits for them, and re-layouts  3.29 us

profile of v7, /device:TPU:1, one launch (start us, length us, event | category | flops | bytes accessed | tf_op | source)
XLA Modules:
  0.0 90.6 jit_solution(10738771083295242546)
XLA Ops:
  0.0 0.0 copy-start.2
  0.0 0.7 copy-done.2
  0.7 0.1 fusion
  0.8 0.0 copy-start.4
  0.8 0.6 copy-done.4
  1.5 0.2 select_reduce_fusion
  1.6 0.1 copy.13
  1.7 0.0 copy-start
  1.7 0.1 reduce-window.8
  1.8 0.0 copy-start.1
  1.8 0.1 add_reduce_fusion
  1.9 0.1 select_reduce_fusion.2.active_ref
  2.1 0.0 copy-start.3
  2.1 0.1 select_reduce_fusion.1
  2.2 0.4 copy-done.3
  2.6 0.1 add_convert_fusion
  2.7 0.7 broadcast_in_dim.60.numbers_ref
  3.3 0.0 copy-done
  3.3 0.0 copy-done.1
  3.3 0.7 pad_maximum_fusion.factor_ref
  4.0 85.1 %sublayer.1 = bf16[32,1536]{1,0:T(8,128)(2,1)} custom-call(bf16[32,1536]{1,0:T(8,128)(2,1)} %stream_ref.1, f32[1536]{0:T(1024)} %gain_ref.1, f32[48,128]{1,0:T(8,128)} %broadcast_in_dim.60.numbers_ref, bf16[4,32,1536]{2,1,0:T(8,128)(2,1)} %gate_in_ref.1, bf16[4,16,1536]{2,1,0:T(8,128)(2,1)} %down_out_ref.1, bf16[4,48,144]{2,1,0:T(8,128)(2,1)} %pad_maximum_fusion.factor_ref, ...), custom_call_target="tpu_custom_call" | custom-call | tf_op jit(solution)/shard_map/sublayer/pallas_call | solution.py:490
  89.1 1.5 %copy.15 = bf16[32,1536]{1,0:T(8,128)(2,1)} copy(bf16[32,1536]{1,0:T(8,128)(2,1)} %sublayer.1) | data formatting | bytes 196608
  (1 shorter events, 0.0 us)
Async XLA Ops:
  0.0 0.7 copy-start.2
  0.8 0.7 copy-start.4
  1.7 1.6 %copy-start = (bf16[4,2,16,144]{3,2,1,0:T(8,128)(2,1)S(1)}, bf16[4,2,16,144]{3,2,1,0:T(8,128)(2,1)}, u32[]{:S(2)}) copy-start(bf16[4,2,16,144]{3,2,1,0:T(8,128)(2,1)} %param.15) | copy-start | bytes 110596
  1.8 1.5 %copy-start.1 = (bf16[4,144,16]{1,2,0:T(8,128)(2,1)S(1)}, bf16[4,144,16]{1,2,0:T(8,128)(2,1)}, u32[]{:S(2)}) copy-start(bf16[4,144,16]{1,2,0:T(8,128)(2,1)} %param.16) | copy-start | bytes 55300
  2.1 0.5 copy-start.3

commit v8 on v7

--- a/solution.py
+++ b/solution.py
@@ -474,9 +474,8 @@
         settle(PICKS)
         compute(4, first_base)
         for far in range(3, -1, -1):
-            base = base_of(far)
+            compute(far, base_of(far))
             pass_on(far + 1)
-            compute(far, base)
         pass_on(0)
         remote(cross_out_ref, cross_in_ref, sum_across_send, sum_across_recv, blk_across).wait_recv()
         total = totals[OWN] + cross_in_ref[...].astype(jnp.float32)

time: 90.8 us -> 88.9 us (0.979)
  the two profiles are of different devices: /device:TPU:1 before, /device:TPU:6 now
where the time goes in v8:
time: 88.9 us; the launch traced here: 88.7 us
  Pallas kernels  83.2 us (94%)
  local copies, waits for them, and re-layouts  4.06 us (5%)
  other arithmetic  1.43 us (2%)
    pallas_call x1, Pallas kernels, sublayer(): pl.pallas_call(kernel, out_shape=jax.ShapeDtypeStruct(block, kind), in_sp...  83.2 us
    unnamed x11, local copies, waits for them, and re-layouts  3.29 us

profile of v8, /device:TPU:6, one launch (start us, length us, event | category | flops | bytes accessed | tf_op | source)
XLA Modules:
  0.0 88.7 jit_solution(16465171264162915393)
XLA Ops:
  0.0 0.0 copy-start.2
  0.0 0.7 copy-done.2
  0.7 0.1 fusion
  0.8 0.0 copy-start.4
  0.8 0.6 copy-done.4
  1.5 0.2 select_reduce_fusion
  1.6 0.1 copy.13
  1.7 0.0 copy-start
  1.7 0.1 reduce-window.8
  1.8 0.0 copy-start.1
  1.8 0.1 add_reduce_fusion
  1.9 0.1 select_reduce_fusion.2.active_ref
  2.1 0.0 copy-start.3
  2.1 0.1 select_reduce_fusion.1
  2.2 0.4 copy-done.3
  2.6 0.1 add_convert_fusion
  2.7 0.7 broadcast_in_dim.60.numbers_ref
  3.3 0.0 copy-done
  3.3 0.0 copy-done.1
  3.3 0.7 pad_maximum_fusion.factor_ref
  4.0 83.2 %sublayer.1 = bf16[32,1536]{1,0:T(8,128)(2,1)} custom-call(bf16[32,1536]{1,0:T(8,128)(2,1)} %stream_ref.1, f32[1536]{0:T(1024)} %gain_ref.1, f32[48,128]{1,0:T(8,128)} %broadcast_in_dim.60.numbers_ref, bf16[4,32,1536]{2,1,0:T(8,128)(2,1)} %gate_in_ref.1, bf16[4,16,1536]{2,1,0:T(8,128)(2,1)} %down_out_ref.1, bf16[4,48,144]{2,1,0:T(8,128)(2,1)} %pad_maximum_fusion.factor_ref, ...), custom_call_target="tpu_custom_call" | custom-call | tf_op jit(solution)/shard_map/sublayer/pallas_call | solution.py:489
  87.2 1.5 %copy.15 = bf16[32,1536]{1,0:T(8,128)(2,1)} copy(bf16[32,1536]{1,0:T(8,128)(2,1)} %sublayer.1) | data formatting | bytes 196608
  (1 shorter events, 0.0 us)
Async XLA Ops:
  0.0 0.7 copy-start.2
  0.8 0.7 copy-start.4
  1.7 1.6 %copy-start = (bf16[4,2,16,144]{3,2,1,0:T(8,128)(2,1)S(1)}, bf16[4,2,16,144]{3,2,1,0:T(8,128)(2,1)}, u32[]{:S(2)}) copy-start(bf16[4,2,16,144]{3,2,1,0:T(8,128)(2,1)} %param.15) | copy-start | bytes 110596
  1.8 1.5 %copy-start.1 = (bf16[4,144,16]{1,2,0:T(8,128)(2,1)S(1)}, bf16[4,144,16]{1,2,0:T(8,128)(2,1)}, u32[]{:S(2)}) copy-start(bf16[4,144,16]{1,2,0:T(8,128)(2,1)} %param.16) | copy-start | bytes 55300
  2.1 0.5 copy-start.3
